TPU v7x, 128 devices: a whole 4x4x4 slice. The times are simulated.
128 devices in a mesh: lat: 8 (over y, core), lon: 16 (over x, z).
Axes of the slice: x: 4, y: 4, z: 4, core: 2. Of those that a mesh axis runs over, the one named last changes fastest.
Arguments:
- field: bfloat16 [128, 256, 384], P('lat', 'lon'), may hold values from -6 to 6
- obs_jac: bfloat16 [128, 128, 128, 384], P(None, ('lat', 'lon')), may hold values from -0.3125 to 0.3125
- obs_frac: bfloat16 [128, 128, 2, 128], P(None, ('lat', 'lon')), may hold values from 0 to 1
- obs_innov: bfloat16 [128, 128, 128], P(None, ('lat', 'lon')), may hold values from -6 to 6
- obs_rinv: bfloat16 [128, 128, 128], P(None, ('lat', 'lon')), may hold values from 1 to 16
- obs_cells: int32 [128, 128, 128], P(None, ('lat', 'lon')), may hold values from -1 to 270, as said below
Outputs:
- departures: float32 [128, 128, 128], P(None, ('lat', 'lon'))
- field_grad: float32 [128, 256, 384], P('lat', 'lon')
Inputs may be any that keep to these rules, and one draw needn't show every extreme that they name: `obs_cells`: in block (o, p) the live slots come first, at least one and at most 128; a live slot holds r * 17 + q with r below 16 and q below 16; slot 0 of every block holds the cell at r = 15, q = 15; the number of live slots varies by owner.
All inputs are finite; a program needn't handle non-finite values.
Results may differ from a plain program's by a relative error of at most 0.0046.
Values may be sent and summed in bfloat16 or wider, within the bound.
No kernel may reach another device: no remote copies, remote signals or barrier semaphores. Data moves between devices by JAX's collectives and lax.ppermute only.
A program may use at most 128 MiB of HBM per device.

v0:
```python
import jax
import jax.numpy as jnp
from jax import lax
from jax.sharding import PartitionSpec as P


def shifted(block, axis, distance):
    devices = range(lax.axis_size(axis))
    route = [(i - distance, i) for i in devices if i - distance in devices]
    return lax.ppermute(block, axis, route)


def passed_along(value, axis, steps):
    count = lax.axis_size(axis)
    pairs = [(source, (source + steps) % count) for source in range(count)]
    return lax.ppermute(value, axis, pairs)


def bilinear_weights(frac_lat, frac_lon):
    lat_part = frac_lat.astype(jnp.float32)
    lon_part = frac_lon.astype(jnp.float32)
    raw_weights = (
        (1.0 - lat_part) * (1.0 - lon_part),
        lat_part * (1.0 - lon_part),
        (1.0 - lat_part) * lon_part,
        lat_part * lon_part,
    )
    return lax.optimization_barrier(tuple((weight.astype(jnp.bfloat16) for weight in raw_weights)))


def spread_matrix(cell_ids, frac_lat, frac_lon, stride, cells_total):
    is_live = cell_ids >= 0
    corner = jnp.where(is_live, cell_ids, 0)
    weights = bilinear_weights(frac_lat, frac_lon)
    cell_axis = lax.broadcasted_iota(jnp.int32, (1, cells_total), 1)
    matrix = jnp.zeros((cell_ids.shape[0], cells_total), jnp.float32)
    for weight, offset in zip(weights, (0, stride, 1, stride + 1)):
        live_weight = jnp.where(is_live, weight.astype(jnp.float32), 0.0)
        matrix = matrix + jnp.where(
            corner[:, None] + offset == cell_axis, live_weight[:, None], 0.0
        )
    return matrix.astype(jnp.bfloat16)


def forward_piece(spread, col_table, cell_ids, innovation, jacobian):
    interp = jnp.dot(spread, col_table, preferred_element_type=jnp.float32)
    evolved = jnp.sum(interp * jacobian.astype(jnp.float32), axis=1)
    return jnp.where(
        cell_ids >= 0, evolved - innovation.astype(jnp.float32), jnp.zeros((), jnp.float32)
    )


def adjoint_piece(spread, inv_error, departure, jacobian, grad_ext):
    contrib = (
        (inv_error.astype(jnp.float32) * departure)[:, None] * jacobian.astype(jnp.float32)
    ).astype(jnp.bfloat16)
    return grad_ext + lax.dot_general(
        spread, contrib, (((0,), (0,)), ((), ())), preferred_element_type=jnp.float32
    )


def shards(field, obs_jac, obs_frac, obs_innov, obs_rinv, obs_cells):
    lat_rows, lon_cols, width_all = field.shape
    north_row = shifted(field[:1], "lat", -1)
    taller = jnp.concatenate([field, north_row], axis=0)
    east_col = passed_along(taller[:, :1], "lon", -1)
    widened = jnp.concatenate([taller, east_col], axis=1)
    stride = lon_cols + 1
    col_table = widened.reshape(-1, width_all)
    cells_total = col_table.shape[0]
    jac_rows, frac_pair, innov_vals, rinv_vals = (
        lax.all_to_all(obs_jac, ("lat", "lon"), split_axis=0, concat_axis=1, tiled=True),
        lax.all_to_all(obs_frac, ("lat", "lon"), split_axis=0, concat_axis=1, tiled=True),
        lax.all_to_all(obs_innov, ("lat", "lon"), split_axis=0, concat_axis=1, tiled=True),
        lax.all_to_all(obs_rinv, ("lat", "lon"), split_axis=0, concat_axis=1, tiled=True),
    )
    cell_vals = lax.all_to_all(obs_cells, ("lat", "lon"), split_axis=0, concat_axis=1, tiled=True)
    sources = cell_vals.shape[1]
    slots_all = cell_vals.shape[2]
    cells_two = cell_vals.reshape(sources, slots_all)
    frac_three = frac_pair.reshape(sources, 2, slots_all)
    innov_two = innov_vals.reshape(sources, slots_all)
    rinv_two = rinv_vals.reshape(sources, slots_all)
    jac_three = jac_rows.reshape(sources, slots_all, width_all)
    piece = slots_all // 8
    piece_rows = sources * piece

    def take_piece(piece_idx):
        start = piece_idx * piece
        cells_p = lax.dynamic_slice_in_dim(cells_two, start, piece, 1).reshape(-1)
        frac_p = lax.dynamic_slice_in_dim(frac_three, start, piece, 2)
        lat_p = frac_p[:, 0, :].reshape(-1)
        lon_p = frac_p[:, 1, :].reshape(-1)
        innov_p = lax.dynamic_slice_in_dim(innov_two, start, piece, 1).reshape(-1)
        rinv_p = lax.dynamic_slice_in_dim(rinv_two, start, piece, 1).reshape(-1)
        jac_p = lax.dynamic_slice_in_dim(jac_three, start, piece, 1).reshape(piece_rows, width_all)
        return (cells_p, lat_p, lon_p, innov_p, rinv_p, jac_p)

    def store_piece(departs, departure, piece_idx):
        return lax.dynamic_update_slice_in_dim(
            departs, departure.reshape(sources, piece), piece_idx * piece, 1
        )

    def full_turn(piece_idx, state_pair):
        grad_ext, departs = state_pair
        cells_p, lat_p, lon_p, innov_p, rinv_p, jac_p = take_piece(piece_idx)
        spread = spread_matrix(cells_p, lat_p, lon_p, stride, cells_total)
        departure = forward_piece(spread, col_table, cells_p, innov_p, jac_p)
        grad_ext = adjoint_piece(spread, rinv_p, departure, jac_p, grad_ext)
        return (grad_ext, store_piece(departs, departure, piece_idx))

    grad_start = jnp.zeros((cells_total, width_all), jnp.float32)
    depart_start = jnp.zeros((sources, slots_all), jnp.float32)
    grad_ext, departs = lax.fori_loop(0, 8, full_turn, (grad_start, depart_start))
    grad_grid = grad_ext.reshape(lat_rows + 1, stride, width_all)
    east_back = passed_along(grad_grid[:, lon_cols:], "lon", 1)
    grad_grid = grad_grid[:, :lon_cols].at[:, :1].add(east_back)
    north_back = shifted(grad_grid[lat_rows:], "lat", 1)
    field_grad = grad_grid[:lat_rows].at[:1].add(north_back)
    departures = lax.all_to_all(
        departs.reshape(1, sources, slots_all),
        ("lat", "lon"),
        split_axis=1,
        concat_axis=0,
        tiled=True,
    )
    return (departures, field_grad)


def solution(mesh):
    placed = (
        P("lat", "lon", None),
        P(None, ("lat", "lon"), None, None),
        P(None, ("lat", "lon"), None, None),
        P(None, ("lat", "lon"), None),
        P(None, ("lat", "lon"), None),
        P(None, ("lat", "lon"), None),
    )
    return jax.shard_map(
        shards,
        mesh=mesh,
        in_specs=placed,
        out_specs=(P(None, ("lat", "lon"), None), P("lat", "lon", None)),
        check_vma=False,
    )
```

profile of v0, /device:TPU:1, one launch (start us, length us, event | category | flops | bytes accessed | tf_op | source)
XLA Modules:
  0.0 425.6 jit_solution(11205427673159762087)
XLA Ops:
  0.6 1.4 copy.22
  2.1 11.5 %all-to-all-start.4 = ((bf16[128,1,128]{2,1,0:T(2,128)(2,1)}), bf16[128,1,128]{2,1,0:T(2,128)(2,1)S(1)}, u32[]{:S(2)}, u32[]{:S(2)}) async-start(bf16[128,1,128]{2,1,0:T(2,128)(2,1)} %copy.22), calls=%async_computation.4 | async-start | bytes 131072 | tf_op jit(solution)/shard_map/all_to_all | solution.py:74
  14.4 8.6 %all-to-all-done.4 = bf16[128,1,128]{2,1,0:T(2,128)(2,1)S(1)} async-done(((bf16[128,1,128]{2,1,0:T(2,128)(2,1)}), bf16[128,1,128]{2,1,0:T(2,128)(2,1)S(1)}, u32[]{:S(2)}, u32[]{:S(2)}) %all-to-all-start.4) | async-done | bytes 32800 | tf_op jit(solution)/shard_map/all_to_all | solution.py:74
  23.0 13.9 %all_to_all.27 = bf16[128,1,128]{2,1,0:T(2,128)(2,1)S(1)} all-to-all(bf16[128,1,128]{2,1,0:T(2,128)(2,1)S(1)} %copy.21), channel_id=1, replica_groups=mesh['lat'=8,'lon'=16] {'lat','lon'}, dimensions={0} | all-to-all | bytes 65536 | tf_op jit(solution)/shard_map/all_to_all | solution.py:75
  36.9 14.2 %all_to_all.28 = s32[128,1,128]{2,1,0:T(1,128)S(1)} all-to-all(s32[128,1,128]{2,1,0:T(1,128)} %param.17), channel_id=1, replica_groups=mesh['lat'=8,'lon'=16] {'lat','lon'}, dimensions={0} | all-to-all | bytes 131072 | tf_op jit(solution)/shard_map/all_to_all | solution.py:77
  51.1 14.2 %all_to_all.29 = bf16[128,1,2,128]{3,2,1,0:T(2,128)(2,1)S(1)} all-to-all(bf16[128,1,2,128]{3,2,1,0:T(2,128)(2,1)} %param.14), channel_id=1, replica_groups=mesh['lat'=8,'lon'=16] {'lat','lon'}, dimensions={0} | all-to-all | bytes 131072 | tf_op jit(solution)/shard_map/all_to_all | solution.py:73
  65.3 5.8 %all-to-all-start.3 = ((bf16[128,1,128,384]{3,2,1,0:T(8,128)(2,1)}), bf16[128,1,128,384]{3,2,1,0:T(8,128)(2,1)}, u32[]{:S(2)}, u32[]{:S(2)}) async-start(bf16[128,1,128,384]{3,2,1,0:T(8,128)(2,1)} %param.13), calls=%async_computation.3 | async-start | bytes 25165824 | tf_op jit(solution)/shard_map/all_to_all | solution.py:72
  71.2 3.2 collective-permute-start
  74.4 151.2 %collective-permute-done = bf16[1,16,384]{2,1,0:T(8,128)(2,1)S(1)} collective-permute-done((bf16[1,16,384]{2,1,0:T(8,128)(2,1)S(1)}, bf16[1,16,384]{2,1,0:T(8,128)(2,1)S(1)}, u32[]{:S(2)}, u32[]{:S(2)}) %collective-permute-start) | collective-permute-done | bytes 12320 | tf_op jit(solution)/shard_map/ppermute | solution.py:10
  225.6 10.0 %collective-permute-start.1 = (bf16[17,1,384]{2,1,0:T(2,128)(2,1)S(1)}, bf16[17,1,384]{2,1,0:T(2,128)(2,1)S(1)}, u32[]{:S(2)}, u32[]{:S(2)}) collective-permute-start(bf16[17,1,384]{2,1,0:T(2,128)(2,1)S(1)} %slice.92), channel_id=1, source_target_pairs={{0,15},{1,0},{2,1},{3,2},{4,3},{5,4},{6,5},{7,6},{8,7},{9,8},{10,9... | collective-permute-start | bytes 39176 | tf_op jit(solution)/shard_map/ppermute | solution.py:16
  239.0 159.9 %while.18 = (s32[]{:T(128)}, f32[289,384]{1,0:T(8,128)}, f32[128,128]{1,0:T(8,128)}, s32[128,128]{1,0:T(8,128)S(1)}, bf16[128,2,128]{2,1,0:T(2,128)(2,1)S(1)}, /...) while((s32[]{:T(128)}, f32[289,384]{1,0:T(8,128)}, ...), condition=%wide.region_2.3_spmd.clone, body=%wide.region_0.2_spmd.clone.sunk | while | flops 927542016 | bytes 22667320 | solution.py:114
  239.7 1.6 constant_dynamic-slice_fusion.7
  241.7 2.3 copy.39
  244.0 7.6 %multiply_reduce_fusion.2 = f32[2048]{0:T(1024)S(1)} fusion(f32[2048,384]{0,1:T(8,128)} %copy.39, bf16[289,384]{1,0:T(8,128)(2,1)} %get-tuple-element.415, f32[2048]{0:T(1024)S(1)} %get-tuple-element.372, s32[2048]{0:T(1024)S(1)} %get-tuple-element.374, f32[2048]{0:T(1024)S(1)} %get-tuple-element.375, s32[2048]{0:T(1024)S(1)} %get-tuple-element.376, ...), kind=kOutput, calls=%fused_computation.1.clone.1 | convolution fusion | flops 463230976 | bytes 3441408 | tf_op jit(solution)/shard_map/while/body/eval_jaxpr/dot_general | solution.py:46
  251.9 5.4 %fusion.10 = f32[289,384]{1,0:T(8,128)} fusion(f32[2048,384]{1,0:T(8,128)S(1)} %bitcast_convert_fusion.2, f32[2048]{0:T(1024)S(1)} %select_multiply_fusion.2, f32[2048]{0:T(1024)S(1)} %get-tuple-element.372, s32[2048]{0:T(1024)S(1)} %get-tuple-element.374, f32[2048]{0:T(1024)S(1)} %get-tuple-element.375, s32[2048]{0:T(1024)S(1)} %get-tuple-element.376, ...), kind=kOutput, calls=%fused_computation.10.clone.1 | convolution fusion | flops 463454976 | bytes 4107265 | tf_op jit(solution)/shard_map/while/body/eval_jaxpr/dot_general | solution.py:57
  259.2 1.6 constant_dynamic-slice_fusion.7
  261.2 2.3 copy.39
  263.5 7.6 %multiply_reduce_fusion.2 = f32[2048]{0:T(1024)S(1)} fusion(f32[2048,384]{0,1:T(8,128)} %copy.39, bf16[289,384]{1,0:T(8,128)(2,1)} %get-tuple-element.415, f32[2048]{0:T(1024)S(1)} %get-tuple-element.372, s32[2048]{0:T(1024)S(1)} %get-tuple-element.374, f32[2048]{0:T(1024)S(1)} %get-tuple-element.375, s32[2048]{0:T(1024)S(1)} %get-tuple-element.376, ...), kind=kOutput, calls=%fused_computation.1.clone.1 | convolution fusion | flops 463230976 | bytes 3441408 | tf_op jit(solution)/shard_map/while/body/eval_jaxpr/dot_general | solution.py:46
  271.4 5.7 %fusion.10 = f32[289,384]{1,0:T(8,128)} fusion(f32[2048,384]{1,0:T(8,128)S(1)} %bitcast_convert_fusion.2, f32[2048]{0:T(1024)S(1)} %select_multiply_fusion.2, f32[2048]{0:T(1024)S(1)} %get-tuple-element.372, s32[2048]{0:T(1024)S(1)} %get-tuple-element.374, f32[2048]{0:T(1024)S(1)} %get-tuple-element.375, s32[2048]{0:T(1024)S(1)} %get-tuple-element.376, ...), kind=kOutput, calls=%fused_computation.10.clone.1 | convolution fusion | flops 463454976 | bytes 4107265 | tf_op jit(solution)/shard_map/while/body/eval_jaxpr/dot_general | solution.py:57
  279.3 1.6 constant_dynamic-slice_fusion.7
  281.2 2.3 copy.39
  283.6 7.6 %multiply_reduce_fusion.2 = f32[2048]{0:T(1024)S(1)} fusion(f32[2048,384]{0,1:T(8,128)} %copy.39, bf16[289,384]{1,0:T(8,128)(2,1)} %get-tuple-element.415, f32[2048]{0:T(1024)S(1)} %get-tuple-element.372, s32[2048]{0:T(1024)S(1)} %get-tuple-element.374, f32[2048]{0:T(1024)S(1)} %get-tuple-element.375, s32[2048]{0:T(1024)S(1)} %get-tuple-element.376, ...), kind=kOutput, calls=%fused_computation.1.clone.1 | convolution fusion | flops 463230976 | bytes 3441408 | tf_op jit(solution)/shard_map/while/body/eval_jaxpr/dot_general | solution.py:46
  291.5 5.7 %fusion.10 = f32[289,384]{1,0:T(8,128)} fusion(f32[2048,384]{1,0:T(8,128)S(1)} %bitcast_convert_fusion.2, f32[2048]{0:T(1024)S(1)} %select_multiply_fusion.2, f32[2048]{0:T(1024)S(1)} %get-tuple-element.372, s32[2048]{0:T(1024)S(1)} %get-tuple-element.374, f32[2048]{0:T(1024)S(1)} %get-tuple-element.375, s32[2048]{0:T(1024)S(1)} %get-tuple-element.376, ...), kind=kOutput, calls=%fused_computation.10.clone.1 | convolution fusion | flops 463454976 | bytes 4107265 | tf_op jit(solution)/shard_map/while/body/eval_jaxpr/dot_general | solution.py:57
  299.3 1.6 constant_dynamic-slice_fusion.7
  301.3 2.3 copy.39
  303.6 7.6 %multiply_reduce_fusion.2 = f32[2048]{0:T(1024)S(1)} fusion(f32[2048,384]{0,1:T(8,128)} %copy.39, bf16[289,384]{1,0:T(8,128)(2,1)} %get-tuple-element.415, f32[2048]{0:T(1024)S(1)} %get-tuple-element.372, s32[2048]{0:T(1024)S(1)} %get-tuple-element.374, f32[2048]{0:T(1024)S(1)} %get-tuple-element.375, s32[2048]{0:T(1024)S(1)} %get-tuple-element.376, ...), kind=kOutput, calls=%fused_computation.1.clone.1 | convolution fusion | flops 463230976 | bytes 3441408 | tf_op jit(solution)/shard_map/while/body/eval_jaxpr/dot_general | solution.py:46
  311.5 5.7 %fusion.10 = f32[289,384]{1,0:T(8,128)} fusion(f32[2048,384]{1,0:T(8,128)S(1)} %bitcast_convert_fusion.2, f32[2048]{0:T(1024)S(1)} %select_multiply_fusion.2, f32[2048]{0:T(1024)S(1)} %get-tuple-element.372, s32[2048]{0:T(1024)S(1)} %get-tuple-element.374, f32[2048]{0:T(1024)S(1)} %get-tuple-element.375, s32[2048]{0:T(1024)S(1)} %get-tuple-element.376, ...), kind=kOutput, calls=%fused_computation.10.clone.1 | convolution fusion | flops 463454976 | bytes 4107265 | tf_op jit(solution)/shard_map/while/body/eval_jaxpr/dot_general | solution.py:57
  319.4 1.6 constant_dynamic-slice_fusion.7
  321.3 2.3 copy.39
  323.7 7.6 %multiply_reduce_fusion.2 = f32[2048]{0:T(1024)S(1)} fusion(f32[2048,384]{0,1:T(8,128)} %copy.39, bf16[289,384]{1,0:T(8,128)(2,1)} %get-tuple-element.415, f32[2048]{0:T(1024)S(1)} %get-tuple-element.372, s32[2048]{0:T(1024)S(1)} %get-tuple-element.374, f32[2048]{0:T(1024)S(1)} %get-tuple-element.375, s32[2048]{0:T(1024)S(1)} %get-tuple-element.376, ...), kind=kOutput, calls=%fused_computation.1.clone.1 | convolution fusion | flops 463230976 | bytes 3441408 | tf_op jit(solution)/shard_map/while/body/eval_jaxpr/dot_general | solution.py:46
  331.6 5.8 %fusion.10 = f32[289,384]{1,0:T(8,128)} fusion(f32[2048,384]{1,0:T(8,128)S(1)} %bitcast_convert_fusion.2, f32[2048]{0:T(1024)S(1)} %select_multiply_fusion.2, f32[2048]{0:T(1024)S(1)} %get-tuple-element.372, s32[2048]{0:T(1024)S(1)} %get-tuple-element.374, f32[2048]{0:T(1024)S(1)} %get-tuple-element.375, s32[2048]{0:T(1024)S(1)} %get-tuple-element.376, ...), kind=kOutput, calls=%fused_computation.10.clone.1 | convolution fusion | flops 463454976 | bytes 4107265 | tf_op jit(solution)/shard_map/while/body/eval_jaxpr/dot_general | solution.py:57
  339.4 1.6 constant_dynamic-slice_fusion.7
  341.4 2.3 copy.39
  343.7 7.6 %multiply_reduce_fusion.2 = f32[2048]{0:T(1024)S(1)} fusion(f32[2048,384]{0,1:T(8,128)} %copy.39, bf16[289,384]{1,0:T(8,128)(2,1)} %get-tuple-element.415, f32[2048]{0:T(1024)S(1)} %get-tuple-element.372, s32[2048]{0:T(1024)S(1)} %get-tuple-element.374, f32[2048]{0:T(1024)S(1)} %get-tuple-element.375, s32[2048]{0:T(1024)S(1)} %get-tuple-element.376, ...), kind=kOutput, calls=%fused_computation.1.clone.1 | convolution fusion | flops 463230976 | bytes 3441408 | tf_op jit(solution)/shard_map/while/body/eval_jaxpr/dot_general | solution.py:46
  351.6 5.8 %fusion.10 = f32[289,384]{1,0:T(8,128)} fusion(f32[2048,384]{1,0:T(8,128)S(1)} %bitcast_convert_fusion.2, f32[2048]{0:T(1024)S(1)} %select_multiply_fusion.2, f32[2048]{0:T(1024)S(1)} %get-tuple-element.372, s32[2048]{0:T(1024)S(1)} %get-tuple-element.374, f32[2048]{0:T(1024)S(1)} %get-tuple-element.375, s32[2048]{0:T(1024)S(1)} %get-tuple-element.376, ...), kind=kOutput, calls=%fused_computation.10.clone.1 | convolution fusion | flops 463454976 | bytes 4107265 | tf_op jit(solution)/shard_map/while/body/eval_jaxpr/dot_general | solution.py:57
  359.5 1.6 constant_dynamic-slice_fusion.7
  361.4 2.3 copy.39
  363.8 7.6 %multiply_reduce_fusion.2 = f32[2048]{0:T(1024)S(1)} fusion(f32[2048,384]{0,1:T(8,128)} %copy.39, bf16[289,384]{1,0:T(8,128)(2,1)} %get-tuple-element.415, f32[2048]{0:T(1024)S(1)} %get-tuple-element.372, s32[2048]{0:T(1024)S(1)} %get-tuple-element.374, f32[2048]{0:T(1024)S(1)} %get-tuple-element.375, s32[2048]{0:T(1024)S(1)} %get-tuple-element.376, ...), kind=kOutput, calls=%fused_computation.1.clone.1 | convolution fusion | flops 463230976 | bytes 3441408 | tf_op jit(solution)/shard_map/while/body/eval_jaxpr/dot_general | solution.py:46
  371.7 5.8 %fusion.10 = f32[289,384]{1,0:T(8,128)} fusion(f32[2048,384]{1,0:T(8,128)S(1)} %bitcast_convert_fusion.2, f32[2048]{0:T(1024)S(1)} %select_multiply_fusion.2, f32[2048]{0:T(1024)S(1)} %get-tuple-element.372, s32[2048]{0:T(1024)S(1)} %get-tuple-element.374, f32[2048]{0:T(1024)S(1)} %get-tuple-element.375, s32[2048]{0:T(1024)S(1)} %get-tuple-element.376, ...), kind=kOutput, calls=%fused_computation.10.clone.1 | convolution fusion | flops 463454976 | bytes 4107265 | tf_op jit(solution)/shard_map/while/body/eval_jaxpr/dot_general | solution.py:57
  379.5 1.6 constant_dynamic-slice_fusion.7
  381.5 2.3 copy.39
  383.8 7.6 %multiply_reduce_fusion.2 = f32[2048]{0:T(1024)S(1)} fusion(f32[2048,384]{0,1:T(8,128)} %copy.39, bf16[289,384]{1,0:T(8,128)(2,1)} %get-tuple-element.415, f32[2048]{0:T(1024)S(1)} %get-tuple-element.372, s32[2048]{0:T(1024)S(1)} %get-tuple-element.374, f32[2048]{0:T(1024)S(1)} %get-tuple-element.375, s32[2048]{0:T(1024)S(1)} %get-tuple-element.376, ...), kind=kOutput, calls=%fused_computation.1.clone.1 | convolution fusion | flops 463230976 | bytes 3441408 | tf_op jit(solution)/shard_map/while/body/eval_jaxpr/dot_general | solution.py:46
  391.7 5.8 %fusion.10 = f32[289,384]{1,0:T(8,128)} fusion(f32[2048,384]{1,0:T(8,128)S(1)} %bitcast_convert_fusion.2, f32[2048]{0:T(1024)S(1)} %select_multiply_fusion.2, f32[2048]{0:T(1024)S(1)} %get-tuple-element.372, s32[2048]{0:T(1024)S(1)} %get-tuple-element.374, f32[2048]{0:T(1024)S(1)} %get-tuple-element.375, s32[2048]{0:T(1024)S(1)} %get-tuple-element.376, ...), kind=kOutput, calls=%fused_computation.10.clone.1 | convolution fusion | flops 463454976 | bytes 4107265 | tf_op jit(solution)/shard_map/while/body/eval_jaxpr/dot_general | solution.py:57
  398.9 1.1 reshape.221
  400.1 6.0 %collective-permute-done.2 = f32[17,1,384]{2,1,0:T(1,128)S(1)} collective-permute-done((f32[17,1,384]{2,1,0:T(1,128)S(1)}, f32[17,1,384]{2,1,0:T(1,128)S(1)}, u32[]{:S(2)}, u32[]{:S(2)}) %collective-permute-start.2) | collective-permute-done | bytes 26144 | tf_op jit(solution)/shard_map/ppermute | solution.py:16
  406.3 3.9 collective-permute-start.3
  410.2 5.2 %all-to-all-start.5 = ((f32[1,128,128]{2,0,1:T(1,128)}), f32[1,128,128]{2,0,1:T(1,128)S(1)}, u32[]{:S(2)}, u32[]{:S(2)}) async-start(f32[1,128,128]{2,0,1:T(1,128)} %bitcast.30), calls=%async_computation.5 | async-start | bytes 131072 | tf_op jit(solution)/shard_map/all_to_all | solution.py:120
  415.4 9.5 %all-to-all-done.5 = f32[1,128,128]{2,0,1:T(1,128)S(1)} async-done(((f32[1,128,128]{2,0,1:T(1,128)}), f32[1,128,128]{2,0,1:T(1,128)S(1)}, u32[]{:S(2)}, u32[]{:S(2)}) %all-to-all-start.5) | async-done | bytes 65568 | tf_op jit(solution)/shard_map/all_to_all | solution.py:120
  (227 shorter events, 26.0 us)
Async XLA Ops:
  2.1 21.0 %all-to-all-start.4 = ((bf16[128,1,128]{2,1,0:T(2,128)(2,1)}), bf16[128,1,128]{2,1,0:T(2,128)(2,1)S(1)}, u32[]{:S(2)}, u32[]{:S(2)}) async-start(bf16[128,1,128]{2,1,0:T(2,128)(2,1)} %copy.22), calls=%async_computation.4 | async-start | bytes 131072 | tf_op jit(solution)/shard_map/all_to_all | solution.py:74
  65.3 5.8 %copy-start.3 = (bf16[16,16,384]{2,1,0:T(8,128)(2,1)S(1)}, bf16[16,16,384]{2,1,0:T(8,128)(2,1)}, u32[]{:S(2)}) copy-start(bf16[16,16,384]{2,1,0:T(8,128)(2,1)} %param.12) | copy-start | bytes 589828
  65.3 173.1 %all-to-all-start.3 = ((bf16[128,1,128,384]{3,2,1,0:T(8,128)(2,1)}), bf16[128,1,128,384]{3,2,1,0:T(8,128)(2,1)}, u32[]{:S(2)}, u32[]{:S(2)}) async-start(bf16[128,1,128,384]{3,2,1,0:T(8,128)(2,1)} %param.13), calls=%async_computation.3 | async-start | bytes 25165824 | tf_op jit(solution)/shard_map/all_to_all | solution.py:72
  71.2 154.4 %collective-permute-start = (bf16[1,16,384]{2,1,0:T(8,128)(2,1)S(1)}, bf16[1,16,384]{2,1,0:T(8,128)(2,1)S(1)}, u32[]{:S(2)}, u32[]{:S(2)}) collective-permute-start(bf16[1,16,384]{2,1,0:T(8,128)(2,1)S(1)} %slice.82), channel_id=1, source_target_pairs={{16,0},{32,16},{48,32},{64,48},{80,64},{96,80},{112,96},{17,1},{33... | collective-permute-start | bytes 36872 | tf_op jit(solution)/shard_map/ppermute | solution.py:10
  225.6 10.9 %collective-permute-start.1 = (bf16[17,1,384]{2,1,0:T(2,128)(2,1)S(1)}, bf16[17,1,384]{2,1,0:T(2,128)(2,1)S(1)}, u32[]{:S(2)}, u32[]{:S(2)}) collective-permute-start(bf16[17,1,384]{2,1,0:T(2,128)(2,1)S(1)} %slice.92), channel_id=1, source_target_pairs={{0,15},{1,0},{2,1},{3,2},{4,3},{5,4},{6,5},{7,6},{8,7},{9,8},{10,9... | collective-permute-start | bytes 39176 | tf_op jit(solution)/shard_map/ppermute | solution.py:16
  239.6 4.4 %copy-start.4 = (f32[2048]{0:T(1024)}, f32[2048]{0:T(1024)S(1)}, u32[]{:S(2)}) copy-start(f32[2048]{0:T(1024)S(1)} %get-tuple-element.379) | copy-start | bytes 24580 | tf_op jit(solution)/shard_map/while
  251.9 5.6 %copy-start.1 = (f32[128,128]{1,0:T(8,128)S(1)}, f32[128,128]{1,0:T(8,128)}, u32[]{:S(2)}) copy-start(f32[128,128]{1,0:T(8,128)} %get-tuple-element.397) | copy-start | bytes 196612 | tf_op jit(solution)/shard_map/while
  257.9 0.6 copy-start.2
  259.2 4.4 %copy-start.4 = (f32[2048]{0:T(1024)}, f32[2048]{0:T(1024)S(1)}, u32[]{:S(2)}) copy-start(f32[2048]{0:T(1024)S(1)} %get-tuple-element.379) | copy-start | bytes 24580 | tf_op jit(solution)/shard_map/while
  271.4 6.0 %copy-start.1 = (f32[128,128]{1,0:T(8,128)S(1)}, f32[128,128]{1,0:T(8,128)}, u32[]{:S(2)}) copy-start(f32[128,128]{1,0:T(8,128)} %get-tuple-element.397) | copy-start | bytes 196612 | tf_op jit(solution)/shard_map/while
  278.0 0.6 copy-start.2
  279.2 4.4 %copy-start.4 = (f32[2048]{0:T(1024)}, f32[2048]{0:T(1024)S(1)}, u32[]{:S(2)}) copy-start(f32[2048]{0:T(1024)S(1)} %get-tuple-element.379) | copy-start | bytes 24580 | tf_op jit(solution)/shard_map/while
  291.5 6.0 %copy-start.1 = (f32[128,128]{1,0:T(8,128)S(1)}, f32[128,128]{1,0:T(8,128)}, u32[]{:S(2)}) copy-start(f32[128,128]{1,0:T(8,128)} %get-tuple-element.397) | copy-start | bytes 196612 | tf_op jit(solution)/shard_map/while
  298.0 0.6 copy-start.2
  299.3 4.4 %copy-start.4 = (f32[2048]{0:T(1024)}, f32[2048]{0:T(1024)S(1)}, u32[]{:S(2)}) copy-start(f32[2048]{0:T(1024)S(1)} %get-tuple-element.379) | copy-start | bytes 24580 | tf_op jit(solution)/shard_map/while
  311.5 5.9 %copy-start.1 = (f32[128,128]{1,0:T(8,128)S(1)}, f32[128,128]{1,0:T(8,128)}, u32[]{:S(2)}) copy-start(f32[128,128]{1,0:T(8,128)} %get-tuple-element.397) | copy-start | bytes 196612 | tf_op jit(solution)/shard_map/while
  318.1 0.6 copy-start.2
  319.3 4.4 %copy-start.4 = (f32[2048]{0:T(1024)}, f32[2048]{0:T(1024)S(1)}, u32[]{:S(2)}) copy-start(f32[2048]{0:T(1024)S(1)} %get-tuple-element.379) | copy-start | bytes 24580 | tf_op jit(solution)/shard_map/while
  331.6 6.0 %copy-start.1 = (f32[128,128]{1,0:T(8,128)S(1)}, f32[128,128]{1,0:T(8,128)}, u32[]{:S(2)}) copy-start(f32[128,128]{1,0:T(8,128)} %get-tuple-element.397) | copy-start | bytes 196612 | tf_op jit(solution)/shard_map/while
  338.1 0.6 copy-start.2
  339.4 4.4 %copy-start.4 = (f32[2048]{0:T(1024)}, f32[2048]{0:T(1024)S(1)}, u32[]{:S(2)}) copy-start(f32[2048]{0:T(1024)S(1)} %get-tuple-element.379) | copy-start | bytes 24580 | tf_op jit(solution)/shard_map/while
  351.6 6.0 %copy-start.1 = (f32[128,128]{1,0:T(8,128)S(1)}, f32[128,128]{1,0:T(8,128)}, u32[]{:S(2)}) copy-start(f32[128,128]{1,0:T(8,128)} %get-tuple-element.397) | copy-start | bytes 196612 | tf_op jit(solution)/shard_map/while
  358.2 0.6 copy-start.2
  359.4 4.4 %copy-start.4 = (f32[2048]{0:T(1024)}, f32[2048]{0:T(1024)S(1)}, u32[]{:S(2)}) copy-start(f32[2048]{0:T(1024)S(1)} %get-tuple-element.379) | copy-start | bytes 24580 | tf_op jit(solution)/shard_map/while
  371.7 6.0 %copy-start.1 = (f32[128,128]{1,0:T(8,128)S(1)}, f32[128,128]{1,0:T(8,128)}, u32[]{:S(2)}) copy-start(f32[128,128]{1,0:T(8,128)} %get-tuple-element.397) | copy-start | bytes 196612 | tf_op jit(solution)/shard_map/while
  378.2 0.6 copy-start.2
  379.5 4.4 %copy-start.4 = (f32[2048]{0:T(1024)}, f32[2048]{0:T(1024)S(1)}, u32[]{:S(2)}) copy-start(f32[2048]{0:T(1024)S(1)} %get-tuple-element.379) | copy-start | bytes 24580 | tf_op jit(solution)/shard_map/while
  391.7 6.0 %copy-start.1 = (f32[128,128]{1,0:T(8,128)S(1)}, f32[128,128]{1,0:T(8,128)}, u32[]{:S(2)}) copy-start(f32[128,128]{1,0:T(8,128)} %get-tuple-element.397) | copy-start | bytes 196612 | tf_op jit(solution)/shard_map/while
  398.3 0.6 copy-start.2
  400.0 6.1 %collective-permute-start.2 = (f32[17,1,384]{2,1,0:T(1,128)S(1)}, f32[17,1,384]{2,1,0:T(1,128)S(1)}, u32[]{:S(2)}, u32[]{:S(2)}) collective-permute-start(f32[17,1,384]{2,1,0:T(1,128)S(1)} %slice.95), channel_id=1, source_target_pairs={{0,1},{1,2},{2,3},{3,4},{4,5},{5,6},{6,7},{7,8},{8,9},{9,10},{10,1... | collective-permute-start | bytes 78344 | tf_op jit(solution)/shard_map/ppermute | solution.py:16
  406.3 9.1 %collective-permute-start.3 = (f32[1,16,384]{2,1,0:T(8,128)S(1)}, f32[1,16,384]{2,1,0:T(8,128)S(1)}, u32[]{:S(2)}, u32[]{:S(2)}) collective-permute-start(f32[1,16,384]{2,1,0:T(8,128)S(1)} %slice.98), channel_id=1, source_target_pairs={{0,16},{16,32},{32,48},{48,64},{64,80},{80,96},{96,112},{1,17},{17... | collective-permute-start | bytes 73736 | tf_op jit(solution)/shard_map/ppermute | solution.py:10
  410.2 14.8 %all-to-all-start.5 = ((f32[1,128,128]{2,0,1:T(1,128)}), f32[1,128,128]{2,0,1:T(1,128)S(1)}, u32[]{:S(2)}, u32[]{:S(2)}) async-start(f32[1,128,128]{2,0,1:T(1,128)} %bitcast.30), calls=%async_computation.5 | async-start | bytes 131072 | tf_op jit(solution)/shard_map/all_to_all | solution.py:120
  415.4 10.2 %copy-start = (f32[16,16,384]{2,1,0:T(8,128)}, f32[16,16,384]{2,1,0:T(8,128)S(1)}, u32[]{:S(2)}) copy-start(f32[16,16,384]{2,1,0:T(8,128)S(1)} %fusion.5) | copy-start | bytes 1179652
where the time goes:
time: 428 us; the launch traced here: 426 us
  waiting for transfers between devices  177 us (41%)
  matrix products  107 us (25%)
  local copies, waits for them, and re-layouts  53 us (12%)
  blocking collectives  42.3 us (10%)
  starting transfers between devices  39.6 us (9%)
  other arithmetic  4.93 us (1%)
    ppermute x2, waiting for transfers between devices, shifted(): return lax.ppermute(block, axis, route)  151 us
    dot_general x8, matrix products, forward_piece(): interp = jnp.dot(spread, col_table, preferred_element_type=jnp.float32)  60.9 us
    dot_general x8, matrix products, adjoint_piece(): lax.dot_general(spread, contrib, (((0,), (0,)), ((), ())), preferred_elem...  45.7 us
    convert_element_type x8, local copies, waits for them, and re-layouts, forward_piece(): evolved = jnp.sum(interp * jacobian.astype(jnp.float32), axis=1)  18.8 us
    all_to_all x1, blocking collectives, shards(): lax.all_to_all(obs_frac, ('lat', 'lon'), split_axis=0, concat_axis=1, til...  14.2 us
    all_to_all x1, blocking collectives, shards(): lax.all_to_all(obs_cells, ('lat', 'lon'), split_axis=0, concat_axis=1, ti...  14.2 us
    all_to_all x1, blocking collectives, shards(): lax.all_to_all(obs_rinv, ('lat', 'lon'), split_axis=0, concat_axis=1, til...  13.9 us
    dynamic_slice x8, local copies, waits for them, and re-layouts, take_piece(): lax.dynamic_slice_in_dim(jac_three, start, piece, 1)  12.7 us
  transfers between devices with their start and end apart: 7, of which 6 were waited for; matrix products, arithmetic and copies ran while one was open for 0% of the time, Pallas kernels for 0%

commit v1 on v0

v1 whole, which is shorter than its diff:
```python
import functools

import jax
import jax.numpy as jnp
from jax import lax
from jax.experimental import pallas as pl
from jax.experimental.pallas import tpu as pltpu
from jax.sharding import PartitionSpec as P

FIRST_SLOTS = 104
TILE = 256
BLOCK = 1024


def shifted(block, axis, distance):
    devices = range(lax.axis_size(axis))
    route = [(i - distance, i) for i in devices if i - distance in devices]
    return lax.ppermute(block, axis, route)


def passed_along(value, axis, steps):
    count = lax.axis_size(axis)
    pairs = [(source, (source + steps) % count) for source in range(count)]
    return lax.ppermute(value, axis, pairs)


def passed_diagonally(value, steps):
    rows, cols = lax.axis_size("lat"), lax.axis_size("lon")
    pairs = [
        (i * cols + j, (i + steps) * cols + (j + steps) % cols)
        for i in range(rows)
        for j in range(cols)
        if 0 <= i + steps < rows
    ]
    return lax.ppermute(value, ("lat", "lon"), pairs)


def exchanged(block):
    return lax.all_to_all(block, ("lat", "lon"), split_axis=0, concat_axis=0, tiled=True)


def chunk_kernel(table, jac, meta, grad_in, depart, grad_out, spread, *, side):
    east = (side + 1) * side
    rows = table.shape[0] - east

    @pl.when(pl.program_id(0) == 0)
    def _():
        grad_out[...] = grad_in[...]

    place = lax.broadcasted_iota(jnp.int32, (rows, TILE), 0).astype(jnp.float32)
    for start in range(0, jac.shape[0], TILE):
        lanes = slice(start, start + TILE)
        frac_lat, frac_lon, innov, rinv, row, col = (meta[i : i + 1, lanes] for i in range(6))
        lat_part = jnp.where(
            place == row, 1.0 - frac_lat, jnp.where(place == row + 1.0, frac_lat, 0.0)
        )
        lon_part = jnp.where(
            place == col, 1.0 - frac_lon, jnp.where(place == col + 1.0, frac_lon, 0.0)
        )
        proj = lax.dot_general(
            table[...],
            jac[lanes, :],
            (((1,), (1,)), ((), ())),
            preferred_element_type=jnp.float32,
        )
        bands = [
            (lat_part[i : i + 1] * lon_part[:side]).astype(jnp.bfloat16) for i in range(side + 1)
        ]
        edge = (lon_part[side : side + 1] * lat_part).astype(jnp.bfloat16)
        total = jnp.zeros((side, TILE), jnp.float32)
        for i, band in enumerate(bands):
            total = total + band.astype(jnp.float32) * proj[i * side : (i + 1) * side]
        edge_total = edge.astype(jnp.float32) * proj[east:]
        evolved = jnp.sum(total, axis=0, keepdims=True) + jnp.sum(edge_total, axis=0, keepdims=True)
        departure = jnp.where(row >= 0.0, evolved - innov, 0.0)
        depart[0, :, lanes] = departure
        scale = rinv * departure
        for i, band in enumerate(bands):
            spread[i * side : (i + 1) * side, lanes] = (band.astype(jnp.float32) * scale).astype(
                jnp.bfloat16
            )
        spread[east:, lanes] = (edge.astype(jnp.float32) * scale).astype(jnp.bfloat16)
    grad_out[...] += jnp.dot(spread[...], jac[...], preferred_element_type=jnp.float32)


def run_chunk(table, jac, meta, grad_in, side):
    slots, width = jac.shape
    cells = table.shape[0]
    steps = slots // BLOCK
    depart, grad = pl.pallas_call(
        functools.partial(chunk_kernel, side=side),
        grid=(steps,),
        in_specs=[
            pl.BlockSpec((cells, width), lambda i: (0, 0)),
            pl.BlockSpec((BLOCK, width), lambda i: (i, 0)),
            pl.BlockSpec((8, BLOCK), lambda i: (0, i)),
            pl.BlockSpec((cells, width), lambda i: (0, 0)),
        ],
        out_specs=[
            pl.BlockSpec((1, 1, BLOCK), lambda i: (i, 0, 0)),
            pl.BlockSpec((cells, width), lambda i: (0, 0)),
        ],
        out_shape=[
            jax.ShapeDtypeStruct((steps, 1, BLOCK), jnp.float32),
            jax.ShapeDtypeStruct((cells, width), jnp.float32),
        ],
        scratch_shapes=[pltpu.VMEM((cells, BLOCK), jnp.bfloat16)],
        compiler_params=pltpu.CompilerParams(
            dimension_semantics=("arbitrary",), vmem_limit_bytes=40 << 20
        ),
    )(table, jac, meta, grad_in)
    return depart, grad


def shards(field, obs_jac, obs_frac, obs_innov, obs_rinv, obs_cells):
    side, _, width = field.shape
    stride = side + 1
    owners, _, slots, _ = obs_jac.shape
    cells = obs_cells.reshape(owners, slots)
    row = jnp.where(cells >= 0, cells // stride, -8)
    col = jnp.where(cells >= 0, cells % stride, -8)
    low = jnp.bfloat16
    meta = jnp.stack(
        [
            obs_frac[:, 0, 0],
            obs_frac[:, 0, 1],
            obs_innov[:, 0],
            obs_rinv[:, 0],
            row.astype(low),
            col.astype(low),
            jnp.zeros((owners, slots), low),
            jnp.zeros((owners, slots), low),
        ],
        axis=1,
    )
    meta = exchanged(meta)
    jac = obs_jac.reshape(owners, slots, width)
    first = exchanged(jac[:, :FIRST_SLOTS])
    second = exchanged(jac[:, FIRST_SLOTS:])

    north = shifted(field[0], "lat", -1)
    east = passed_along(field[:, 0], "lon", -1)
    corner = passed_diagonally(field[0, :1], -1)
    pad = jnp.zeros((side - 1, width), field.dtype)
    table = jnp.concatenate([field.reshape(side * side, width), north, east, corner, pad], axis=0)

    fields = meta.transpose(1, 0, 2).astype(jnp.float32)
    meta_first = fields[:, :, :FIRST_SLOTS].reshape(8, -1)
    meta_second = fields[:, :, FIRST_SLOTS:].reshape(8, -1)
    grad = jnp.zeros(table.shape, jnp.float32)
    depart_first, grad = run_chunk(table, first.reshape(-1, width), meta_first, grad, side)
    depart_second, grad = run_chunk(table, second.reshape(-1, width), meta_second, grad, side)

    departs = jnp.concatenate(
        [depart_first.reshape(owners, -1), depart_second.reshape(owners, -1)], axis=1
    )
    main = side * side
    grid = grad[:main].reshape(side, side, width)
    north_back = shifted(grad[main : main + side], "lat", 1)
    east_back = passed_along(grad[main + side : main + 2 * side], "lon", 1)
    corner_back = passed_diagonally(grad[main + 2 * side : main + 2 * side + 1], 1)
    departures = exchanged(departs[:, None, :])
    top = north_back + jnp.pad(corner_back, ((0, side - 1), (0, 0)))
    field_grad = grid.at[:, 0].add(east_back).at[0].add(top)
    return (departures, field_grad)


def solution(mesh):
    placed = (
        P("lat", "lon", None),
        P(None, ("lat", "lon"), None, None),
        P(None, ("lat", "lon"), None, None),
        P(None, ("lat", "lon"), None),
        P(None, ("lat", "lon"), None),
        P(None, ("lat", "lon"), None),
    )
    return jax.shard_map(
        shards,
        mesh=mesh,
        in_specs=placed,
        out_specs=(P(None, ("lat", "lon"), None), P("lat", "lon", None)),
        check_vma=False,
    )
```

time: 428 us -> 254 us (0.59)
  matrix products: 107 us -> 0 us
  blocking collectives: 42.3 us -> 0 us
  waiting for transfers between devices: 177 us -> 149 us
  local copies, waits for them, and re-layouts: 53 us -> 25.6 us
  starting transfers between devices: 39.6 us -> 57.8 us
  Pallas kernels: 0 us -> 17 us
    ppermute x2, waiting for transfers between devices: 151 us -> 0.01 us  [shifted(): return lax.ppermute(block, axis, route)]
    all_to_all x3 -> x4, waiting for transfers between devices: 19.2 us -> 135 us  [exchanged(): lax.all_to_all(block, ('lat', 'lon'), split_axis=0, concat_axis=0, tiled=...]
    dot_general x16 -> x0, matrix products: 107 us -> none  [the longest x8 60.9 us: forward_piece(): interp = jnp.dot(spread, col_table, preferred_element_type=jnp.float32)]
    all_to_all x3 -> x0, blocking collectives: 42.3 us -> none  [the longest x1 14.2 us: shards(): lax.all_to_all(obs_frac, ('lat', 'lon'), split_axis=0, concat_axis=1, til...]
    convert_element_type x40 -> x0, local copies, waits for them, and re-layouts: 21.3 us -> none  [the longest x8 18.8 us: forward_piece(): evolved = jnp.sum(interp * jacobian.astype(jnp.float32), axis=1)]
    all_to_all x3 -> x4, starting transfers between devices: 22.5 us -> 42.3 us  [exchanged(): lax.all_to_all(block, ('lat', 'lon'), split_axis=0, concat_axis=0, tiled=...]
    pallas_call x0 -> x2, Pallas kernels: none -> 17 us  [run_chunk(): pl.pallas_call(functools.partial(chunk_kernel, side=side), grid=(steps,),...]
    slice x14 -> x10, local copies, waits for them, and re-layouts: 1.86 us -> 17 us  [the longest x1 8.73 us: shards(): first = exchanged(jac[:, :FIRST_SLOTS])]
  transfers between devices with their start and end apart: 7 -> 10, of which waited for: 6 -> 4; matrix products, arithmetic and copies ran while one was open for 0% -> 8% of each run, Pallas kernels for 0% -> 6%
where the time goes in v1:
time: 254 us; the launch traced here: 253 us
  waiting for transfers between devices  149 us (59%)
  starting transfers between devices  57.8 us (23%)
  local copies, waits for them, and re-layouts  25.6 us (10%)
  Pallas kernels  17 us (7%)
    all_to_all x4, waiting for transfers between devices, exchanged(): lax.all_to_all(block, ('lat', 'lon'), split_axis=0, concat_axis=0, tiled=...  135 us
    all_to_all x4, starting transfers between devices, exchanged(): lax.all_to_all(block, ('lat', 'lon'), split_axis=0, concat_axis=0, tiled=...  42.3 us
    pallas_call x2, Pallas kernels, run_chunk(): pl.pallas_call(functools.partial(chunk_kernel, side=side), grid=(steps,),...  17 us
    ppermute x2, waiting for transfers between devices, passed_diagonally(): return lax.ppermute(value, ('lat', 'lon'), pairs)  14.5 us
    slice x1, local copies, waits for them, and re-layouts, shards(): first = exchanged(jac[:, :FIRST_SLOTS])  8.73 us
    ppermute x2, starting transfers between devices, passed_along(): return lax.ppermute(value, axis, pairs)  7.27 us
  transfers between devices with their start and end apart: 10, of which 4 were waited for; matrix products, arithmetic and copies ran while one was open for 8% of the time, Pallas kernels for 6%

profile of v1, /device:TPU:1, one launch (start us, length us, event | category | flops | bytes accessed | tf_op | source)
XLA Modules:
  0.0 253.0 jit_solution(11611625496380542025)
XLA Ops:
  0.6 1.0 fusion.4
  1.7 0.1 copy.20
  1.7 0.1 copy.21
  1.8 1.5 fusion.1
  3.3 0.8 copy.22
  4.1 0.8 copy.23
  4.9 1.4 stack.9
  6.3 11.5 %all-to-all-start.1 = ((bf16[128,8,128]{2,1,0:T(8,128)(2,1)}), bf16[128,8,128]{2,1,0:T(8,128)(2,1)S(1)}, u32[]{:S(2)}, u32[]{:S(2)}) async-start(bf16[128,8,128]{2,1,0:T(8,128)(2,1)} %stack.9), calls=%async_computation.1 | async-start | bytes 524288 | tf_op jit(solution)/shard_map/all_to_all | solution.py:39
  17.8 8.7 %slice.98 = bf16[128,104,384]{2,1,0:T(8,128)(2,1)} slice(bf16[128,128,384]{2,1,0:T(8,128)(2,1)} %bitcast.25), slice={[0:128], [0:104], [0:384]} | slice | bytes 20447232 | tf_op jit(solution)/shard_map/slice | solution.py:138
  26.5 2.1 all-to-all-done.1
  28.7 8.0 %all-to-all-start = ((bf16[128,104,384]{2,1,0:T(8,128)(2,1)}), bf16[128,104,384]{2,1,0:T(8,128)(2,1)}, u32[]{:S(2)}, u32[]{:S(2)}) async-start(bf16[128,104,384]{2,1,0:T(8,128)(2,1)} %slice.98), calls=%async_computation | async-start | bytes 20447232 | tf_op jit(solution)/shard_map/all_to_all | solution.py:39
  36.7 3.3 %slice.100 = bf16[128,24,384]{2,1,0:T(8,128)(2,1)} slice(bf16[128,128,384]{2,1,0:T(8,128)(2,1)} %bitcast.26), slice={[0:128], [104:128], [0:384]} | slice | bytes 4718592 | tf_op jit(solution)/shard_map/slice | solution.py:139
  40.0 123.3 %all-to-all-done = bf16[128,104,384]{2,1,0:T(8,128)(2,1)} async-done(((bf16[128,104,384]{2,1,0:T(8,128)(2,1)}), bf16[128,104,384]{2,1,0:T(8,128)(2,1)}, u32[]{:S(2)}, u32[]{:S(2)}) %all-to-all-start) | async-done | bytes 10223648 | tf_op jit(solution)/shard_map/all_to_all | solution.py:39
  163.4 9.8 %all-to-all-start.2 = ((bf16[128,24,384]{2,1,0:T(8,128)(2,1)}), bf16[128,24,384]{2,1,0:T(8,128)(2,1)S(1)}, u32[]{:S(2)}, u32[]{:S(2)}) async-start(bf16[128,24,384]{2,1,0:T(8,128)(2,1)} %slice.100), calls=%async_computation.2 | async-start | bytes 4718592 | tf_op jit(solution)/shard_map/all_to_all | solution.py:39
  173.1 0.0 copy-done.2
  173.2 5.5 %collective-permute-start.1 = (bf16[16,384]{1,0:T(8,128)(2,1)S(1)}, bf16[16,384]{1,0:T(8,128)(2,1)S(1)}, u32[]{:S(2)}, u32[]{:S(2)}) collective-permute-start(bf16[16,384]{1,0:T(8,128)(2,1)S(1)} %bitcast.31), channel_id=1, source_target_pairs={{0,15},{1,0},{2,1},{3,2},{4,3},{5,4},{6,5},{7,6},{8,7},{9,8},{10,9... | collective-permute-start | bytes 36872 | tf_op jit(solution)/shard_map/ppermute | solution.py:24
  178.7 2.5 %collective-permute-start = (bf16[16,384]{1,0:T(8,128)(2,1)S(1)}, bf16[16,384]{1,0:T(8,128)(2,1)S(1)}, u32[]{:S(2)}, u32[]{:S(2)}) collective-permute-start(bf16[16,384]{1,0:T(8,128)(2,1)S(1)} %slice_bitcast_fusion), channel_id=1, source_target_pairs={{16,0},{32,16},{48,32},{64,48},{80,64},{96,80},{112,96},{17,1},{33... | collective-permute-start | bytes 36872 | tf_op jit(solution)/shard_map/ppermute | solution.py:18
  181.2 1.9 collective-permute-start.2
  183.2 14.5 %collective-permute-done.2 = bf16[1,384]{1,0:T(2,128)(2,1)S(1)} collective-permute-done((bf16[1,384]{1,0:T(2,128)(2,1)S(1)}, bf16[1,384]{1,0:T(2,128)(2,1)S(1)}, u32[]{:S(2)}, u32[]{:S(2)}) %collective-permute-start.2) | collective-permute-done | bytes 800 | tf_op jit(solution)/shard_map/ppermute | solution.py:35
  197.7 0.0 collective-permute-done.1
  197.7 0.0 collective-permute-done
  197.7 0.3 concatenate.10.table
  198.1 1.0 slice.101
  199.1 0.9 copy.24
  200.0 1.3 reshape.98.meta
  201.3 1.9 copy.25
  203.3 1.9 reshape.101.meta
  205.3 14.3 %shard_map.77 = (f32[13,1,1024]{2,1,0:T(1,128)S(1)}, f32[304,384]{1,0:T(8,128)S(1)}) custom-call(bf16[304,384]{1,0:T(8,128)(2,1)S(1)} %concatenate.10.table, bf16[13312,384]{1,0:T(8,128)(2,1)} %bitcast.5.jac, f32[8,13312]{1,0:T(8,128)S(1)} %reshape.98.meta, f32[304,384]{1,0:T(8,128)S(1)} %broadcast_in_dim.16.grad_in), custom_call_target="tpu_custom_call" | custom-call | tf_op jit(solution)/shard_map/pallas_call | solution.py:90
  219.6 0.0 all-to-all-done.2
  219.6 0.0 copy-start
  219.6 0.9 copy-done
  220.5 2.7 %shard_map.78 = (f32[3,1,1024]{2,1,0:T(1,128)S(1)}, f32[304,384]{1,0:T(8,128)S(1)}) custom-call(bf16[304,384]{1,0:T(8,128)(2,1)S(1)} %concatenate.10.table, bf16[3072,384]{1,0:T(8,128)(2,1)S(1)} %bitcast.24, f32[8,3072]{1,0:T(8,128)S(1)} %copy-done, f32[304,384]{1,0:T(8,128)S(1)} %get-tuple-element.31.grad_in), custom_call_target="tpu_custom_call" | custom-call | tf_op jit(solution)/shard_map/pallas_call | solution.py:90
  223.2 1.8 collective-permute-start.3
  225.0 1.9 collective-permute-start.4
  227.0 1.9 collective-permute-start.5
  228.9 0.1 reshape.102
  229.0 0.1 reduce.4
  229.2 0.1 reshape.99
  229.3 0.7 pad_maximum_fusion
  230.0 13.0 %all-to-all-start.3 = ((f32[128,1,128]{2,1,0:T(1,128)}), f32[128,1,128]{2,1,0:T(1,128)S(1)}, u32[]{:S(2)}, u32[]{:S(2)}) async-start(f32[128,1,128]{2,1,0:T(1,128)} %bitcast.11), calls=%async_computation.3 | async-start | bytes 131072 | tf_op jit(solution)/shard_map/all_to_all | solution.py:39
  242.9 0.0 collective-permute-done.3
  243.0 0.1 scatter-add.6
  243.1 0.0 collective-permute-done.5
  243.1 0.0 collective-permute-done.4
  243.1 0.0 copy-start.1
  243.2 9.2 %all-to-all-done.3 = f32[128,1,128]{2,1,0:T(1,128)S(1)} async-done(((f32[128,1,128]{2,1,0:T(1,128)}), f32[128,1,128]{2,1,0:T(1,128)S(1)}, u32[]{:S(2)}, u32[]{:S(2)}) %all-to-all-start.3) | async-done | bytes 65568 | tf_op jit(solution)/shard_map/all_to_all | solution.py:39
  252.4 0.6 copy.37
  253.0 0.0 copy-done.1
  (16 shorter events, 0.3 us)
Async XLA Ops:
  6.3 22.4 %all-to-all-start.1 = ((bf16[128,8,128]{2,1,0:T(8,128)(2,1)}), bf16[128,8,128]{2,1,0:T(8,128)(2,1)S(1)}, u32[]{:S(2)}, u32[]{:S(2)}) async-start(bf16[128,8,128]{2,1,0:T(8,128)(2,1)} %stack.9), calls=%async_computation.1 | async-start | bytes 524288 | tf_op jit(solution)/shard_map/all_to_all | solution.py:39
  26.5 146.6 %copy-start.2 = (bf16[16,16,384]{2,1,0:T(8,128)(2,1)S(1)}, bf16[16,16,384]{2,1,0:T(8,128)(2,1)}, u32[]{:S(2)}) copy-start(bf16[16,16,384]{2,1,0:T(8,128)(2,1)} %param.10) | copy-start | bytes 589828
  28.7 134.7 %all-to-all-start = ((bf16[128,104,384]{2,1,0:T(8,128)(2,1)}), bf16[128,104,384]{2,1,0:T(8,128)(2,1)}, u32[]{:S(2)}, u32[]{:S(2)}) async-start(bf16[128,104,384]{2,1,0:T(8,128)(2,1)} %slice.98), calls=%async_computation | async-start | bytes 20447232 | tf_op jit(solution)/shard_map/all_to_all | solution.py:39
  163.4 56.2 %all-to-all-start.2 = ((bf16[128,24,384]{2,1,0:T(8,128)(2,1)}), bf16[128,24,384]{2,1,0:T(8,128)(2,1)S(1)}, u32[]{:S(2)}, u32[]{:S(2)}) async-start(bf16[128,24,384]{2,1,0:T(8,128)(2,1)} %slice.100), calls=%async_computation.2 | async-start | bytes 4718592 | tf_op jit(solution)/shard_map/all_to_all | solution.py:39
  173.2 24.5 %collective-permute-start.1 = (bf16[16,384]{1,0:T(8,128)(2,1)S(1)}, bf16[16,384]{1,0:T(8,128)(2,1)S(1)}, u32[]{:S(2)}, u32[]{:S(2)}) collective-permute-start(bf16[16,384]{1,0:T(8,128)(2,1)S(1)} %bitcast.31), channel_id=1, source_target_pairs={{0,15},{1,0},{2,1},{3,2},{4,3},{5,4},{6,5},{7,6},{8,7},{9,8},{10,9... | collective-permute-start | bytes 36872 | tf_op jit(solution)/shard_map/ppermute | solution.py:24
  178.7 19.0 %collective-permute-start = (bf16[16,384]{1,0:T(8,128)(2,1)S(1)}, bf16[16,384]{1,0:T(8,128)(2,1)S(1)}, u32[]{:S(2)}, u32[]{:S(2)}) collective-permute-start(bf16[16,384]{1,0:T(8,128)(2,1)S(1)} %slice_bitcast_fusion), channel_id=1, source_target_pairs={{16,0},{32,16},{48,32},{64,48},{80,64},{96,80},{112,96},{17,1},{33... | collective-permute-start | bytes 36872 | tf_op jit(solution)/shard_map/ppermute | solution.py:18
  181.2 16.5 %collective-permute-start.2 = (bf16[1,384]{1,0:T(2,128)(2,1)S(1)}, bf16[1,384]{1,0:T(2,128)(2,1)S(1)}, u32[]{:S(2)}, u32[]{:S(2)}) collective-permute-start(bf16[1,384]{1,0:T(2,128)(2,1)S(1)} %slice_bitcast_fusion.1), channel_id=1, source_target_pairs={{16,15},{17,0},{18,1},{19,2},{20,3},{21,4},{22,5},{23,6},{24,7},{2... | collective-permute-start | bytes 2312 | tf_op jit(solution)/shard_map/ppermute | solution.py:35
  219.6 0.9 copy-start
  223.2 19.7 %collective-permute-start.3 = (f32[16,384]{1,0:T(8,128)S(1)}, f32[16,384]{1,0:T(8,128)S(1)}, u32[]{:S(2)}, u32[]{:S(2)}) collective-permute-start(f32[16,384]{1,0:T(8,128)S(1)} %get-tuple-element.37), channel_id=1, source_target_pairs={{0,1},{1,2},{2,3},{3,4},{4,5},{5,6},{6,7},{7,8},{8,9},{9,10},{10,1... | collective-permute-start | bytes 73736 | tf_op jit(solution)/shard_map/ppermute | solution.py:24
  225.0 18.1 %collective-permute-start.4 = (f32[16,384]{1,0:T(8,128)S(1)}, f32[16,384]{1,0:T(8,128)S(1)}, u32[]{:S(2)}, u32[]{:S(2)}) collective-permute-start(f32[16,384]{1,0:T(8,128)S(1)} %get-tuple-element.36), channel_id=1, source_target_pairs={{0,16},{16,32},{32,48},{48,64},{64,80},{80,96},{96,112},{1,17},{17... | collective-permute-start | bytes 73736 | tf_op jit(solution)/shard_map/ppermute | solution.py:18
  227.0 16.2 %collective-permute-start.5 = (f32[1,384]{1,0:T(1,128)S(1)}, f32[1,384]{1,0:T(1,128)S(1)}, u32[]{:S(2)}, u32[]{:S(2)}) collective-permute-start(f32[1,384]{1,0:T(1,128)S(1)} %slice.97), channel_id=1, source_target_pairs={{0,17},{1,18},{2,19},{3,20},{4,21},{5,22},{6,23},{7,24},{8,25},{9,... | collective-permute-start | bytes 4616 | tf_op jit(solution)/shard_map/ppermute | solution.py:35
  230.0 22.4 %all-to-all-start.3 = ((f32[128,1,128]{2,1,0:T(1,128)}), f32[128,1,128]{2,1,0:T(1,128)S(1)}, u32[]{:S(2)}, u32[]{:S(2)}) async-start(f32[128,1,128]{2,1,0:T(1,128)} %bitcast.11), calls=%async_computation.3 | async-start | bytes 131072 | tf_op jit(solution)/shard_map/all_to_all | solution.py:39
  243.1 9.9 %copy-start.1 = (f32[16,16,384]{2,1,0:T(8,128)}, f32[16,16,384]{2,1,0:T(8,128)S(1)}, u32[]{:S(2)}) copy-start(f32[16,16,384]{2,1,0:T(8,128)S(1)} %fusion.2) | copy-start | bytes 1179652

commit v2 on v1

v2 whole, which is shorter than its diff:
```python
import functools

import jax
import jax.numpy as jnp
from jax import lax
from jax.experimental import pallas as pl
from jax.experimental.pallas import tpu as pltpu
from jax.sharding import PartitionSpec as P

SENDERS = 32


def shifted(block, axis, distance):
    devices = range(lax.axis_size(axis))
    route = [(i - distance, i) for i in devices if i - distance in devices]
    return lax.ppermute(block, axis, route)


def passed_along(value, axis, steps):
    count = lax.axis_size(axis)
    pairs = [(source, (source + steps) % count) for source in range(count)]
    return lax.ppermute(value, axis, pairs)


def passed_diagonally(value, steps):
    rows, cols = lax.axis_size("lat"), lax.axis_size("lon")
    pairs = [
        (i * cols + j, (i + steps) * cols + (j + steps) % cols)
        for i in range(rows)
        for j in range(cols)
        if 0 <= i + steps < rows
    ]
    return lax.ppermute(value, ("lat", "lon"), pairs)


def exchanged(block):
    return lax.all_to_all(block, ("lat", "lon"), split_axis=0, concat_axis=0, tiled=True)


def observe_kernel(table, jac, meta, depart, grad, spread, *, side):
    east = (side + 1) * side
    rows = table.shape[0] - east
    slots = meta.shape[2]
    tile = 2 * slots
    place = lax.broadcasted_iota(jnp.int32, (rows, tile), 0).astype(jnp.float32)
    for pair in range(meta.shape[0] // 2):
        lanes = slice(pair * tile, (pair + 1) * tile)
        fields = jnp.concatenate([meta[2 * pair], meta[2 * pair + 1]], axis=1).astype(jnp.float32)
        frac_lat, frac_lon, innov, rinv, row, col = (fields[i : i + 1] for i in range(6))
        lat_part = jnp.where(
            place == row, 1.0 - frac_lat, jnp.where(place == row + 1.0, frac_lat, 0.0)
        )
        lon_part = jnp.where(
            place == col, 1.0 - frac_lon, jnp.where(place == col + 1.0, frac_lon, 0.0)
        )
        proj = lax.dot_general(
            table[...],
            jac[lanes, :],
            (((1,), (1,)), ((), ())),
            preferred_element_type=jnp.float32,
        )
        bands = [
            (lat_part[i : i + 1] * lon_part[:side]).astype(jnp.bfloat16) for i in range(side + 1)
        ]
        edge = (lon_part[side : side + 1] * lat_part).astype(jnp.bfloat16)
        total = jnp.zeros((side, tile), jnp.float32)
        for i, band in enumerate(bands):
            total = total + band.astype(jnp.float32) * proj[i * side : (i + 1) * side]
        edge_total = edge.astype(jnp.float32) * proj[east:]
        evolved = jnp.sum(total, axis=0, keepdims=True) + jnp.sum(edge_total, axis=0, keepdims=True)
        departure = jnp.where(row >= 0.0, evolved - innov, 0.0)
        depart[2 * pair] = departure[:, :slots]
        depart[2 * pair + 1] = departure[:, slots:]
        scale = rinv * departure
        for i, band in enumerate(bands):
            spread[i * side : (i + 1) * side, lanes] = (band.astype(jnp.float32) * scale).astype(
                jnp.bfloat16
            )
        spread[east:, lanes] = (edge.astype(jnp.float32) * scale).astype(jnp.bfloat16)
    part = jnp.dot(spread[...], jac[...], preferred_element_type=jnp.float32)

    @pl.when(pl.program_id(0) == 0)
    def _():
        grad[...] = part

    @pl.when(pl.program_id(0) > 0)
    def _():
        grad[...] += part


def observe(table, jac, meta, side):
    cells, width = table.shape
    senders, fields, slots = meta.shape
    block = SENDERS * slots
    return pl.pallas_call(
        functools.partial(observe_kernel, side=side),
        grid=(senders // SENDERS,),
        in_specs=[
            pl.BlockSpec((cells, width), lambda i: (0, 0)),
            pl.BlockSpec((block, width), lambda i: (i, 0)),
            pl.BlockSpec((SENDERS, fields, slots), lambda i: (i, 0, 0)),
        ],
        out_specs=[
            pl.BlockSpec((SENDERS, 1, slots), lambda i: (i, 0, 0)),
            pl.BlockSpec((cells, width), lambda i: (0, 0)),
        ],
        out_shape=[
            jax.ShapeDtypeStruct((senders, 1, slots), jnp.float32),
            jax.ShapeDtypeStruct((cells, width), jnp.float32),
        ],
        scratch_shapes=[pltpu.VMEM((cells, block), jnp.bfloat16)],
        compiler_params=pltpu.CompilerParams(
            dimension_semantics=("arbitrary",), vmem_limit_bytes=32 << 20
        ),
    )(table, jac, meta)


def shards(field, obs_jac, obs_frac, obs_innov, obs_rinv, obs_cells):
    side, _, width = field.shape
    stride = side + 1
    owners, _, slots, _ = obs_jac.shape
    jac = exchanged(obs_jac.reshape(owners, slots, width)).reshape(owners * slots, width)
    cells = obs_cells.reshape(owners, slots)
    row = jnp.where(cells >= 0, cells // stride, -8)
    col = jnp.where(cells >= 0, cells % stride, -8)
    low = jnp.bfloat16
    meta = jnp.stack(
        [
            obs_frac[:, 0, 0],
            obs_frac[:, 0, 1],
            obs_innov[:, 0],
            obs_rinv[:, 0],
            row.astype(low),
            col.astype(low),
            jnp.zeros((owners, slots), low),
            jnp.zeros((owners, slots), low),
        ],
        axis=1,
    )
    north = shifted(field[0], "lat", -1)
    east = passed_along(field[:, 0], "lon", -1)
    corner = passed_diagonally(field[0, :1], -1)
    pad = jnp.zeros((side - 1, width), field.dtype)
    table = jnp.concatenate([field.reshape(side * side, width), north, east, corner, pad], axis=0)

    meta, table, jac = lax.optimization_barrier((meta, table, jac))
    meta = exchanged(meta)

    departs, grad = observe(table, jac, meta, side)
    departures = exchanged(departs)
    main = side * side
    grid = grad[:main].reshape(side, side, width)
    north_back = shifted(grad[main : main + side], "lat", 1)
    east_back = passed_along(grad[main + side : main + 2 * side], "lon", 1)
    corner_back = passed_diagonally(grad[main + 2 * side : main + 2 * side + 1], 1)
    top = north_back + jnp.pad(corner_back, ((0, side - 1), (0, 0)))
    field_grad = grid.at[:, 0].add(east_back).at[0].add(top)
    return (departures, field_grad)


def solution(mesh):
    placed = (
        P("lat", "lon", None),
        P(None, ("lat", "lon"), None, None),
        P(None, ("lat", "lon"), None, None),
        P(None, ("lat", "lon"), None),
        P(None, ("lat", "lon"), None),
        P(None, ("lat", "lon"), None),
    )
    return jax.shard_map(
        shards,
        mesh=mesh,
        in_specs=placed,
        out_specs=(P(None, ("lat", "lon"), None), P("lat", "lon", None)),
        check_vma=False,
    )
```

time: 254 us -> 229 us (0.902)
  local copies, waits for them, and re-layouts: 25.6 us -> 2.24 us
  starting transfers between devices: 57.8 us -> 36.4 us
  blocking collectives: 0 us -> 18 us
  waiting for transfers between devices: 149 us -> 157 us
  Pallas kernels: 17 us -> 14 us
    ppermute x2, waiting for transfers between devices: 14.5 us -> 149 us  [passed_diagonally(): return lax.ppermute(value, ('lat', 'lon'), pairs)]
    all_to_all x4 -> x2, waiting for transfers between devices: 135 us -> 8.1 us  [exchanged(): lax.all_to_all(block, ('lat', 'lon'), split_axis=0, concat_axis=0, tiled=...]
    all_to_all x4 -> x2, starting transfers between devices: 42.3 us -> 19.2 us  [exchanged(): lax.all_to_all(block, ('lat', 'lon'), split_axis=0, concat_axis=0, tiled=...]
    all_to_all x0 -> x1, blocking collectives: none -> 18 us  [exchanged(): lax.all_to_all(block, ('lat', 'lon'), split_axis=0, concat_axis=0, tiled=...]
    slice x5 -> x0, local copies, waits for them, and re-layouts: 15.9 us -> none  [the longest x1 8.73 us: shards(): first = exchanged(jac[:, :FIRST_SLOTS])]
    ppermute x2, starting transfers between devices: 3.84 us -> 12.2 us  [passed_diagonally(): return lax.ppermute(value, ('lat', 'lon'), pairs)]
    ppermute x2, starting transfers between devices: 7.27 us -> 0.8 us  [passed_along(): return lax.ppermute(value, axis, pairs)]
    reshape x4 -> x0, local copies, waits for them, and re-layouts: 3.49 us -> none  [the longest x1 1.95 us: shards(): meta_second = fields[:, :, FIRST_SLOTS:].reshape(8, -1)]
  transfers between devices with their start and end apart: 10 -> 8, of which waited for: 4 -> 4; matrix products, arithmetic and copies ran while one was open for 8% -> 1% of each run, Pallas kernels for 6% -> 0%
where the time goes in v2:
time: 229 us
  waiting for transfers between devices  157 us (69%)
  starting transfers between devices  36.4 us (16%)
  blocking collectives  18 us (8%)
  Pallas kernels  14 us (6%)
    ppermute x2, waiting for transfers between devices, passed_diagonally(): return lax.ppermute(value, ('lat', 'lon'), pairs)  149 us
    all_to_all x2, starting transfers between devices, exchanged(): lax.all_to_all(block, ('lat', 'lon'), split_axis=0, concat_axis=0, tiled=...  19.2 us
    all_to_all x1, blocking collectives, exchanged(): lax.all_to_all(block, ('lat', 'lon'), split_axis=0, concat_axis=0, tiled=...  18 us
    pallas_call x1, Pallas kernels, observe(): pl.pallas_call(functools.partial(observe_kernel, side=side), grid=(sender...  14 us
    ppermute x2, starting transfers between devices, passed_diagonally(): return lax.ppermute(value, ('lat', 'lon'), pairs)  12.2 us
    all_to_all x2, waiting for transfers between devices, exchanged(): lax.all_to_all(block, ('lat', 'lon'), split_axis=0, concat_axis=0, tiled=...  8.1 us
  transfers between devices with their start and end apart: 8, of which 4 were waited for; matrix products, arithmetic and copies ran while one was open for 1% of the time, Pallas kernels for 0%

profile of v2, /device:TPU:1, one launch (start us, length us, event | category | flops | bytes accessed | tf_op | source)
XLA Modules:
  0.0 229.2 jit_solution(15363619220762921070)
XLA Ops:
  0.6 0.0 copy-start.1
  0.6 0.0 copy-start.2
  0.7 0.0 copy-start.3
  0.7 0.0 copy-start.4
  0.7 0.0 copy-start.5
  0.7 11.9 %all-to-all-start = ((bf16[128,128,384]{2,1,0:T(8,128)(2,1)}), bf16[128,128,384]{2,1,0:T(8,128)(2,1)}, u32[]{:S(2)}, u32[]{:S(2)}) async-start(bf16[128,128,384]{2,1,0:T(8,128)(2,1)} %bitcast.17), calls=%async_computation | async-start | bytes 25165824 | tf_op jit(solution)/shard_map/all_to_all | solution.py:37
  12.6 0.0 copy-done.1
  12.6 7.6 %collective-permute-start.2 = (bf16[1,384]{1,0:T(2,128)(2,1)S(1)}, bf16[1,384]{1,0:T(2,128)(2,1)S(1)}, u32[]{:S(2)}, u32[]{:S(2)}) collective-permute-start(bf16[1,384]{1,0:T(2,128)(2,1)S(1)} %slice_bitcast_fusion.1), channel_id=1, source_target_pairs={{16,15},{17,0},{18,1},{19,2},{20,3},{21,4},{22,5},{23,6},{24,7},{2... | collective-permute-start | bytes 2312 | tf_op jit(solution)/shard_map/ppermute | solution.py:33
  20.2 1.9 collective-permute-start
  22.2 0.4 collective-permute-start.1
  22.5 0.0 copy-done.2
  22.6 0.1 fusion.4
  22.6 0.0 copy-done.3
  22.7 0.6 fusion.1
  23.3 0.0 copy-done.4
  23.3 0.1 copy.17
  23.4 0.0 copy-done.5
  23.4 0.1 copy.18
  23.5 0.1 copy.16
  23.5 0.1 copy.15
  23.6 0.7 stack.9
  24.4 147.4 %collective-permute-done.2 = bf16[1,384]{1,0:T(2,128)(2,1)S(1)} collective-permute-done((bf16[1,384]{1,0:T(2,128)(2,1)S(1)}, bf16[1,384]{1,0:T(2,128)(2,1)S(1)}, u32[]{:S(2)}, u32[]{:S(2)}) %collective-permute-start.2) | collective-permute-done | bytes 800 | tf_op jit(solution)/shard_map/ppermute | solution.py:33
  171.8 0.0 collective-permute-done
  171.8 0.0 collective-permute-done.1
  171.8 0.3 concatenate.7.table
  172.1 7.2 %all-to-all-done = bf16[128,128,384]{2,1,0:T(8,128)(2,1)} async-done(((bf16[128,128,384]{2,1,0:T(8,128)(2,1)}), bf16[128,128,384]{2,1,0:T(8,128)(2,1)}, u32[]{:S(2)}, u32[]{:S(2)}) %all-to-all-start) | async-done | bytes 12582944 | tf_op jit(solution)/shard_map/all_to_all | solution.py:37
  179.3 18.0 %all_to_all.15.meta = bf16[128,8,128]{2,1,0:T(8,128)(2,1)S(1)} all-to-all(bf16[128,8,128]{2,1,0:T(8,128)(2,1)S(1)} %stack.9), channel_id=1, replica_groups=mesh['lat'=8,'lon'=16] {'lat','lon'}, dimensions={0} | all-to-all | bytes 524288 | tf_op jit(solution)/shard_map/all_to_all | solution.py:37
  197.3 14.0 %shard_map.77 = (f32[128,1,128]{2,1,0:T(1,128)}, f32[304,384]{1,0:T(8,128)S(1)}) custom-call(bf16[304,384]{1,0:T(8,128)(2,1)S(1)} %concatenate.7.table, bf16[16384,384]{1,0:T(8,128)(2,1)} %bitcast.7.jac, bf16[128,8,128]{2,1,0:T(8,128)(2,1)S(1)} %all_to_all.15.meta), custom_call_target="tpu_custom_call" | custom-call | tf_op jit(solution)/shard_map/pallas_call | solution.py:95
  211.3 0.4 collective-permute-start.3
  211.7 7.3 %all-to-all-start.2 = ((f32[128,1,128]{2,1,0:T(1,128)}), f32[128,1,128]{2,1,0:T(1,128)S(1)}, u32[]{:S(2)}, u32[]{:S(2)}) async-start(f32[128,1,128]{2,1,0:T(1,128)} %get-tuple-element.34), calls=%async_computation.2 | async-start | bytes 131072 | tf_op jit(solution)/shard_map/all_to_all | solution.py:37
  219.1 4.6 %collective-permute-start.5 = (f32[1,384]{1,0:T(1,128)S(1)}, f32[1,384]{1,0:T(1,128)S(1)}, u32[]{:S(2)}, u32[]{:S(2)}) collective-permute-start(f32[1,384]{1,0:T(1,128)S(1)} %slice.81), channel_id=1, source_target_pairs={{0,17},{1,18},{2,19},{3,20},{4,21},{5,22},{6,23},{7,24},{8,25},{9,... | collective-permute-start | bytes 4616 | tf_op jit(solution)/shard_map/ppermute | solution.py:33
  223.7 2.2 collective-permute-start.4
  225.9 0.0 collective-permute-done.3
  226.0 0.1 scatter-add.6
  226.1 1.5 collective-permute-done.5
  227.6 0.0 collective-permute-done.4
  227.6 0.0 copy-start
  227.6 0.9 all-to-all-done.2
  228.5 0.6 copy.30
  229.2 0.0 copy-done
  (12 shorter events, 0.1 us)
Async XLA Ops:
  0.6 12.0 %copy-start.1 = (bf16[16,16,384]{2,1,0:T(8,128)(2,1)S(1)}, bf16[16,16,384]{2,1,0:T(8,128)(2,1)}, u32[]{:S(2)}) copy-start(bf16[16,16,384]{2,1,0:T(8,128)(2,1)} %param.10) | copy-start | bytes 589828
  0.6 21.9 %copy-start.2 = (bf16[128,1,2,128]{3,2,1,0:T(2,128)(2,1)S(1)}, bf16[128,1,2,128]{3,2,1,0:T(2,128)(2,1)}, u32[]{:S(2)}) copy-start(bf16[128,1,2,128]{3,2,1,0:T(2,128)(2,1)} %param.12) | copy-start | bytes 196612
  0.7 22.0 %copy-start.3 = (s32[128,1,128]{2,1,0:T(1,128)S(1)}, s32[128,1,128]{2,1,0:T(1,128)}, u32[]{:S(2)}) copy-start(s32[128,1,128]{2,1,0:T(1,128)} %param.15) | copy-start | bytes 196612
  0.7 22.7 %copy-start.4 = (bf16[128,1,128]{2,0,1:T(8,128)(2,1)S(1)}, bf16[128,1,128]{2,0,1:T(8,128)(2,1)}, u32[]{:S(2)}) copy-start(bf16[128,1,128]{2,0,1:T(8,128)(2,1)} %param.13) | copy-start | bytes 98308
  0.7 22.7 %copy-start.5 = (bf16[128,1,128]{2,0,1:T(8,128)(2,1)S(1)}, bf16[128,1,128]{2,0,1:T(8,128)(2,1)}, u32[]{:S(2)}) copy-start(bf16[128,1,128]{2,0,1:T(8,128)(2,1)} %param.14) | copy-start | bytes 98308
  0.7 178.6 %all-to-all-start = ((bf16[128,128,384]{2,1,0:T(8,128)(2,1)}), bf16[128,128,384]{2,1,0:T(8,128)(2,1)}, u32[]{:S(2)}, u32[]{:S(2)}) async-start(bf16[128,128,384]{2,1,0:T(8,128)(2,1)} %bitcast.17), calls=%async_computation | async-start | bytes 25165824 | tf_op jit(solution)/shard_map/all_to_all | solution.py:37
  12.6 159.2 %collective-permute-start.2 = (bf16[1,384]{1,0:T(2,128)(2,1)S(1)}, bf16[1,384]{1,0:T(2,128)(2,1)S(1)}, u32[]{:S(2)}, u32[]{:S(2)}) collective-permute-start(bf16[1,384]{1,0:T(2,128)(2,1)S(1)} %slice_bitcast_fusion.1), channel_id=1, source_target_pairs={{16,15},{17,0},{18,1},{19,2},{20,3},{21,4},{22,5},{23,6},{24,7},{2... | collective-permute-start | bytes 2312 | tf_op jit(solution)/shard_map/ppermute | solution.py:33
  20.2 151.6 %collective-permute-start = (bf16[16,384]{1,0:T(8,128)(2,1)S(1)}, bf16[16,384]{1,0:T(8,128)(2,1)S(1)}, u32[]{:S(2)}, u32[]{:S(2)}) collective-permute-start(bf16[16,384]{1,0:T(8,128)(2,1)S(1)} %slice_bitcast_fusion), channel_id=1, source_target_pairs={{16,0},{32,16},{48,32},{64,48},{80,64},{96,80},{112,96},{17,1},{33... | collective-permute-start | bytes 36872 | tf_op jit(solution)/shard_map/ppermute | solution.py:16
  22.2 149.6 %collective-permute-start.1 = (bf16[16,384]{1,0:T(8,128)(2,1)S(1)}, bf16[16,384]{1,0:T(8,128)(2,1)S(1)}, u32[]{:S(2)}, u32[]{:S(2)}) collective-permute-start(bf16[16,384]{1,0:T(8,128)(2,1)S(1)} %bitcast.21), channel_id=1, source_target_pairs={{0,15},{1,0},{2,1},{3,2},{4,3},{5,4},{6,5},{7,6},{8,7},{9,8},{10,9... | collective-permute-start | bytes 36872 | tf_op jit(solution)/shard_map/ppermute | solution.py:22
  211.3 14.7 %collective-permute-start.3 = (f32[16,384]{1,0:T(8,128)S(1)}, f32[16,384]{1,0:T(8,128)S(1)}, u32[]{:S(2)}, u32[]{:S(2)}) collective-permute-start(f32[16,384]{1,0:T(8,128)S(1)} %get-tuple-element.37), channel_id=1, source_target_pairs={{0,1},{1,2},{2,3},{3,4},{4,5},{5,6},{6,7},{7,8},{8,9},{9,10},{10,1... | collective-permute-start | bytes 73736 | tf_op jit(solution)/shard_map/ppermute | solution.py:22
  211.7 16.8 %all-to-all-start.2 = ((f32[128,1,128]{2,1,0:T(1,128)}), f32[128,1,128]{2,1,0:T(1,128)S(1)}, u32[]{:S(2)}, u32[]{:S(2)}) async-start(f32[128,1,128]{2,1,0:T(1,128)} %get-tuple-element.34), calls=%async_computation.2 | async-start | bytes 131072 | tf_op jit(solution)/shard_map/all_to_all | solution.py:37
  219.1 8.5 %collective-permute-start.5 = (f32[1,384]{1,0:T(1,128)S(1)}, f32[1,384]{1,0:T(1,128)S(1)}, u32[]{:S(2)}, u32[]{:S(2)}) collective-permute-start(f32[1,384]{1,0:T(1,128)S(1)} %slice.81), channel_id=1, source_target_pairs={{0,17},{1,18},{2,19},{3,20},{4,21},{5,22},{6,23},{7,24},{8,25},{9,... | collective-permute-start | bytes 4616 | tf_op jit(solution)/shard_map/ppermute | solution.py:33
  223.7 3.9 %collective-permute-start.4 = (f32[16,384]{1,0:T(8,128)S(1)}, f32[16,384]{1,0:T(8,128)S(1)}, u32[]{:S(2)}, u32[]{:S(2)}) collective-permute-start(f32[16,384]{1,0:T(8,128)S(1)} %get-tuple-element.36), channel_id=1, source_target_pairs={{0,16},{16,32},{32,48},{48,64},{64,80},{80,96},{96,112},{1,17},{17... | collective-permute-start | bytes 73736 | tf_op jit(solution)/shard_map/ppermute | solution.py:16
  227.6 1.6 copy-start

commit v3 on v2

--- a/solution.py
+++ b/solution.py
@@ -35,6 +35,36 @@
 
 def exchanged(block):
     return lax.all_to_all(block, ("lat", "lon"), split_axis=0, concat_axis=0, tiled=True)
+
+
+def metadata_kernel(frac, innov, rinv, cells, meta, *, stride):
+    cell = cells[...].astype(jnp.float32)
+    row = ((cell + 0.5) * (1.0 / stride)).astype(jnp.int32).astype(jnp.float32)
+    col = cell - stride * row
+    live = cell >= 0.0
+    row = jnp.where(live, row, -8.0)
+    col = jnp.where(live, col, -8.0)
+    both = frac[...].astype(jnp.float32)
+    none = jnp.zeros_like(cell)
+    fields = [
+        both[:, 0],
+        both[:, 1],
+        innov[...].astype(jnp.float32),
+        rinv[...].astype(jnp.float32),
+        row,
+        col,
+        none,
+        none,
+    ]
+    meta[...] = jnp.stack(fields, axis=1).astype(meta.dtype)
+
+
+def metadata(frac, innov, rinv, cells, stride):
+    owners, slots = cells.shape
+    return pl.pallas_call(
+        functools.partial(metadata_kernel, stride=stride),
+        out_shape=jax.ShapeDtypeStruct((owners, 8, slots), frac.dtype),
+    )(frac, innov, rinv, cells)
 
 
 def observe_kernel(table, jac, meta, depart, grad, spread, *, side):
@@ -119,42 +149,31 @@
     side, _, width = field.shape
     stride = side + 1
     owners, _, slots, _ = obs_jac.shape
-    jac = exchanged(obs_jac.reshape(owners, slots, width)).reshape(owners * slots, width)
-    cells = obs_cells.reshape(owners, slots)
-    row = jnp.where(cells >= 0, cells // stride, -8)
-    col = jnp.where(cells >= 0, cells % stride, -8)
-    low = jnp.bfloat16
-    meta = jnp.stack(
-        [
-            obs_frac[:, 0, 0],
-            obs_frac[:, 0, 1],
-            obs_innov[:, 0],
-            obs_rinv[:, 0],
-            row.astype(low),
-            col.astype(low),
-            jnp.zeros((owners, slots), low),
-            jnp.zeros((owners, slots), low),
-        ],
-        axis=1,
+    meta = exchanged(
+        metadata(
+            obs_frac.reshape(owners, 2, slots),
+            obs_innov.reshape(owners, slots),
+            obs_rinv.reshape(owners, slots),
+            obs_cells.reshape(owners, slots),
+            stride,
+        )
     )
     north = shifted(field[0], "lat", -1)
-    east = passed_along(field[:, 0], "lon", -1)
-    corner = passed_diagonally(field[0, :1], -1)
+    east = passed_along(jnp.concatenate([field[:, 0], north[:1]], axis=0), "lon", -1)
     pad = jnp.zeros((side - 1, width), field.dtype)
-    table = jnp.concatenate([field.reshape(side * side, width), north, east, corner, pad], axis=0)
-
-    meta, table, jac = lax.optimization_barrier((meta, table, jac))
-    meta = exchanged(meta)
+    table = jnp.concatenate([field.reshape(side * side, width), north, east, pad], axis=0)
+    meta, table, obs_jac = lax.optimization_barrier((meta, table, obs_jac))
+    jac = exchanged(obs_jac.reshape(owners, slots, width)).reshape(owners * slots, width)
 
     departs, grad = observe(table, jac, meta, side)
     departures = exchanged(departs)
     main = side * side
     grid = grad[:main].reshape(side, side, width)
-    north_back = shifted(grad[main : main + side], "lat", 1)
-    east_back = passed_along(grad[main + side : main + 2 * side], "lon", 1)
-    corner_back = passed_diagonally(grad[main + 2 * side : main + 2 * side + 1], 1)
-    top = north_back + jnp.pad(corner_back, ((0, side - 1), (0, 0)))
-    field_grad = grid.at[:, 0].add(east_back).at[0].add(top)
+    east_back = passed_along(grad[main + side : main + 2 * side + 1], "lon", 1)
+    north_row = grad[main : main + side]
+    north_row = north_row + jnp.pad(east_back[side:], ((0, side - 1), (0, 0)))
+    north_back = shifted(north_row, "lat", 1)
+    field_grad = grid.at[:, 0].add(east_back[:side]).at[0].add(north_back)
     return (departures, field_grad)
 
 

time: 229 us -> 209 us (0.913)
  waiting for transfers between devices: 157 us -> 8.98 us
  blocking collectives: 18 us -> 151 us
  starting transfers between devices: 36.4 us -> 30.1 us
    ppermute x2 -> x0, waiting for transfers between devices: 149 us -> none  [passed_diagonally(): return lax.ppermute(value, ('lat', 'lon'), pairs)]
    all_to_all x1, blocking collectives: 18 us -> 151 us  [exchanged(): lax.all_to_all(block, ('lat', 'lon'), split_axis=0, concat_axis=0, tiled=...]
    ppermute x2 -> x0, starting transfers between devices: 12.2 us -> none  [passed_diagonally(): return lax.ppermute(value, ('lat', 'lon'), pairs)]
    ppermute x2, starting transfers between devices: 0.8 us -> 5.49 us  [passed_along(): return lax.ppermute(value, axis, pairs)]
    ppermute x2, starting transfers between devices: 4.15 us -> 6.86 us  [shifted(): return lax.ppermute(block, axis, route)]
  transfers between devices with their start and end apart: 8 -> 6, of which waited for: 4 -> 4; matrix products, arithmetic and copies ran while one was open for 1% -> 1% of each run, Pallas kernels for 0% -> 1%
where the time goes in v3:
time: 209 us
  blocking collectives  151 us (72%)
  starting transfers between devices  30.1 us (14%)
  Pallas kernels  14.2 us (7%)
  waiting for transfers between devices  8.98 us (4%)
  local copies, waits for them, and re-layouts  2.5 us (1%)
    all_to_all x1, blocking collectives, exchanged(): lax.all_to_all(block, ('lat', 'lon'), split_axis=0, concat_axis=0, tiled=...  151 us
    all_to_all x2, starting transfers between devices, exchanged(): lax.all_to_all(block, ('lat', 'lon'), split_axis=0, concat_axis=0, tiled=...  17.8 us
    pallas_call x1, Pallas kernels, observe(): pl.pallas_call(functools.partial(observe_kernel, side=side), grid=(sender...  12.2 us
    all_to_all x2, waiting for transfers between devices, exchanged(): lax.all_to_all(block, ('lat', 'lon'), split_axis=0, concat_axis=0, tiled=...  7.41 us
    ppermute x2, starting transfers between devices, shifted(): return lax.ppermute(block, axis, route)  6.86 us
    ppermute x2, starting transfers between devices, passed_along(): return lax.ppermute(value, axis, pairs)  5.49 us
  transfers between devices with their start and end apart: 6, of which 4 were waited for; matrix products, arithmetic and copies ran while one was open for 1% of the time, Pallas kernels for 1%

profile of v3, /device:TPU:1, one launch (start us, length us, event | category | flops | bytes accessed | tf_op | source)
XLA Modules:
  0.0 208.8 jit_solution(14643633708799842195)
XLA Ops:
  0.6 0.7 slice_bitcast_fusion
  1.3 3.3 %collective-permute-start = (bf16[16,384]{1,0:T(8,128)(2,1)S(1)}, bf16[16,384]{1,0:T(8,128)(2,1)S(1)}, u32[]{:S(2)}, u32[]{:S(2)}) collective-permute-start(bf16[16,384]{1,0:T(8,128)(2,1)S(1)} %slice_bitcast_fusion), channel_id=1, source_target_pairs={{16,0},{32,16},{48,32},{64,48},{80,64},{96,80},{112,96},{17,1},{33... | collective-permute-start | bytes 36872 | tf_op jit(solution)/shard_map/ppermute | solution.py:16
  4.7 2.0 shard_map.77
  6.6 10.2 %all-to-all-start = ((bf16[128,8,128]{2,1,0:T(8,128)(2,1)}), bf16[128,8,128]{2,1,0:T(8,128)(2,1)S(1)}, u32[]{:S(2)}, u32[]{:S(2)}) async-start(bf16[128,8,128]{2,1,0:T(8,128)(2,1)} %shard_map.77), calls=%async_computation | async-start | bytes 524288 | tf_op jit(solution)/shard_map/all_to_all | solution.py:37
  16.8 0.9 slice.69
  17.7 0.0 collective-permute-done
  17.8 5.5 %collective-permute-start.1 = (bf16[17,384]{1,0:T(8,128)(2,1)S(1)}, bf16[17,384]{1,0:T(8,128)(2,1)S(1)}, u32[]{:S(2)}, u32[]{:S(2)}) collective-permute-start(bf16[17,384]{1,0:T(8,128)(2,1)S(1)} %pad_maximum_fusion), channel_id=1, source_target_pairs={{0,15},{1,0},{2,1},{3,2},{4,3},{5,4},{6,5},{7,6},{8,7},{9,8},{10,9... | collective-permute-start | bytes 39176 | tf_op jit(solution)/shard_map/ppermute | solution.py:22
  23.3 0.1 pad.12.clone
  23.3 0.8 collective-permute-done.1
  24.2 1.0 maximum_maximum_fusion.table
  25.2 2.5 %all-to-all-done.meta = bf16[128,8,128]{2,1,0:T(8,128)(2,1)S(1)} async-done(((bf16[128,8,128]{2,1,0:T(8,128)(2,1)}), bf16[128,8,128]{2,1,0:T(8,128)(2,1)S(1)}, u32[]{:S(2)}, u32[]{:S(2)}) %all-to-all-start) | async-done | bytes 262176 | tf_op jit(solution)/shard_map/all_to_all | solution.py:37
  27.7 151.2 %all_to_all.15 = bf16[128,128,384]{2,1,0:T(8,128)(2,1)S(1)} all-to-all(bf16[128,128,384]{2,1,0:T(8,128)(2,1)} %bitcast.16), channel_id=1, replica_groups=mesh['lat'=8,'lon'=16] {'lat','lon'}, dimensions={0} | all-to-all | bytes 25165824 | tf_op jit(solution)/shard_map/all_to_all | solution.py:37
  178.8 12.2 %shard_map.78 = (f32[128,1,128]{2,1,0:T(1,128)}, f32[304,384]{1,0:T(8,128)S(1)}) custom-call(bf16[304,384]{1,0:T(8,128)(2,1)S(1)} %maximum_maximum_fusion.table, bf16[16384,384]{1,0:T(8,128)(2,1)S(1)} %bitcast.15, bf16[128,8,128]{2,1,0:T(8,128)(2,1)S(1)} %all-to-all-done.meta), custom_call_target="tpu_custom_call" | custom-call | tf_op jit(solution)/shard_map/pallas_call | solution.py:125
  191.0 0.0 collective-permute-start.2
  191.1 7.6 %all-to-all-start.2 = ((f32[128,1,128]{2,1,0:T(1,128)}), f32[128,1,128]{2,1,0:T(1,128)S(1)}, u32[]{:S(2)}, u32[]{:S(2)}) async-start(f32[128,1,128]{2,1,0:T(1,128)} %get-tuple-element.34), calls=%async_computation.2 | async-start | bytes 131072 | tf_op jit(solution)/shard_map/all_to_all | solution.py:37
  198.7 0.0 collective-permute-done.2
  198.7 3.5 %collective-permute-start.3 = (f32[16,384]{1,0:T(8,128)S(1)}, f32[16,384]{1,0:T(8,128)S(1)}, u32[]{:S(2)}, u32[]{:S(2)}) collective-permute-start(f32[16,384]{1,0:T(8,128)S(1)} %pad_add_fusion), channel_id=1, source_target_pairs={{0,16},{16,32},{32,48},{48,64},{64,80},{80,96},{96,112},{1,17},{17... | collective-permute-start | bytes 73736 | tf_op jit(solution)/shard_map/ppermute | solution.py:16
  202.3 0.1 scatter-add.6
  202.4 0.8 collective-permute-done.3
  203.2 0.0 copy-start
  203.2 4.9 %all-to-all-done.2 = f32[128,1,128]{2,1,0:T(1,128)S(1)} async-done(((f32[128,1,128]{2,1,0:T(1,128)}), f32[128,1,128]{2,1,0:T(1,128)S(1)}, u32[]{:S(2)}, u32[]{:S(2)}) %all-to-all-start.2) | async-done | bytes 65568 | tf_op jit(solution)/shard_map/all_to_all | solution.py:37
  208.1 0.6 copy.15
  208.8 0.0 copy-done
  (11 shorter events, 0.1 us)
Async XLA Ops:
  1.3 16.4 %collective-permute-start = (bf16[16,384]{1,0:T(8,128)(2,1)S(1)}, bf16[16,384]{1,0:T(8,128)(2,1)S(1)}, u32[]{:S(2)}, u32[]{:S(2)}) collective-permute-start(bf16[16,384]{1,0:T(8,128)(2,1)S(1)} %slice_bitcast_fusion), channel_id=1, source_target_pairs={{16,0},{32,16},{48,32},{64,48},{80,64},{96,80},{112,96},{17,1},{33... | collective-permute-start | bytes 36872 | tf_op jit(solution)/shard_map/ppermute | solution.py:16
  6.6 21.1 %all-to-all-start = ((bf16[128,8,128]{2,1,0:T(8,128)(2,1)}), bf16[128,8,128]{2,1,0:T(8,128)(2,1)S(1)}, u32[]{:S(2)}, u32[]{:S(2)}) async-start(bf16[128,8,128]{2,1,0:T(8,128)(2,1)} %shard_map.77), calls=%async_computation | async-start | bytes 524288 | tf_op jit(solution)/shard_map/all_to_all | solution.py:37
  17.8 6.4 %collective-permute-start.1 = (bf16[17,384]{1,0:T(8,128)(2,1)S(1)}, bf16[17,384]{1,0:T(8,128)(2,1)S(1)}, u32[]{:S(2)}, u32[]{:S(2)}) collective-permute-start(bf16[17,384]{1,0:T(8,128)(2,1)S(1)} %pad_maximum_fusion), channel_id=1, source_target_pairs={{0,15},{1,0},{2,1},{3,2},{4,3},{5,4},{6,5},{7,6},{8,7},{9,8},{10,9... | collective-permute-start | bytes 39176 | tf_op jit(solution)/shard_map/ppermute | solution.py:22
  191.0 7.6 %collective-permute-start.2 = (f32[17,384]{1,0:T(8,128)S(1)}, f32[17,384]{1,0:T(8,128)S(1)}, u32[]{:S(2)}, u32[]{:S(2)}) collective-permute-start(f32[17,384]{1,0:T(8,128)S(1)} %slice.73), channel_id=1, source_target_pairs={{0,1},{1,2},{2,3},{3,4},{4,5},{5,6},{6,7},{7,8},{8,9},{9,10},{10,1... | collective-permute-start | bytes 78344 | tf_op jit(solution)/shard_map/ppermute | solution.py:22
  191.1 17.0 %all-to-all-start.2 = ((f32[128,1,128]{2,1,0:T(1,128)}), f32[128,1,128]{2,1,0:T(1,128)S(1)}, u32[]{:S(2)}, u32[]{:S(2)}) async-start(f32[128,1,128]{2,1,0:T(1,128)} %get-tuple-element.34), calls=%async_computation.2 | async-start | bytes 131072 | tf_op jit(solution)/shard_map/all_to_all | solution.py:37
  198.7 4.5 %collective-permute-start.3 = (f32[16,384]{1,0:T(8,128)S(1)}, f32[16,384]{1,0:T(8,128)S(1)}, u32[]{:S(2)}, u32[]{:S(2)}) collective-permute-start(f32[16,384]{1,0:T(8,128)S(1)} %pad_add_fusion), channel_id=1, source_target_pairs={{0,16},{16,32},{32,48},{48,64},{64,80},{80,96},{96,112},{1,17},{17... | collective-permute-start | bytes 73736 | tf_op jit(solution)/shard_map/ppermute | solution.py:16
  203.2 5.6 %copy-start = (f32[16,16,384]{2,1,0:T(8,128)}, f32[16,16,384]{2,1,0:T(8,128)S(1)}, u32[]{:S(2)}) copy-start(f32[16,16,384]{2,1,0:T(8,128)S(1)} %fusion) | copy-start | bytes 1179652

commit v4 on v3

v4 whole, which is shorter than its diff:
```python
import functools

import jax
import jax.numpy as jnp
from jax import lax
from jax.experimental import pallas as pl
from jax.experimental.pallas import tpu as pltpu
from jax.sharding import PartitionSpec as P

SENDERS = 64
LANES = 128


def shifted(block, axis, distance):
    devices = range(lax.axis_size(axis))
    route = [(i - distance, i) for i in devices if i - distance in devices]
    return lax.ppermute(block, axis, route)


def passed_along(value, axis, steps):
    count = lax.axis_size(axis)
    pairs = [(source, (source + steps) % count) for source in range(count)]
    return lax.ppermute(value, axis, pairs)


def passed_diagonally(value, steps):
    rows, cols = lax.axis_size("lat"), lax.axis_size("lon")
    pairs = [
        (i * cols + j, (i + steps) * cols + (j + steps) % cols)
        for i in range(rows)
        for j in range(cols)
        if 0 <= i + steps < rows
    ]
    return lax.ppermute(value, ("lat", "lon"), pairs)


def exchanged(block):
    return lax.all_to_all(block, ("lat", "lon"), split_axis=0, concat_axis=0, tiled=True)


def pack_kernel(jac, frac, innov, rinv, cells, packed, sems, *, stride):
    owners, slots, width = jac.shape
    groups, strips = sems.shape
    group = owners // groups
    copies = [
        pltpu.make_async_copy(
            jac.at[pl.ds(i * group, group), :, pl.ds(j * LANES, LANES)],
            packed.at[pl.ds(i * group, group), pl.ds(j * slots, slots)],
            sems.at[i, j],
        )
        for i in range(groups)
        for j in range(strips)
    ]
    for copy in copies:
        copy.start()
    cell = cells[...].astype(jnp.float32)
    row = ((cell + 0.5) * (1.0 / stride)).astype(jnp.int32).astype(jnp.float32)
    col = cell - stride * row
    live = cell >= 0.0
    row = jnp.where(live, row, -8.0)
    col = jnp.where(live, col, -8.0)
    both = frac[...].astype(jnp.float32)
    none = jnp.zeros_like(cell)
    fields = [
        both[:, 0],
        both[:, 1],
        innov[...].astype(jnp.float32),
        rinv[...].astype(jnp.float32),
        row,
        col,
        none,
        none,
    ]
    packed[:, strips * slots :] = jnp.stack(fields, axis=1).astype(packed.dtype)
    for copy in copies:
        copy.wait()


def pack(jac, frac, innov, rinv, cells, stride):
    owners, slots, width = jac.shape
    strips = width // LANES
    return pl.pallas_call(
        functools.partial(pack_kernel, stride=stride),
        in_specs=[pl.BlockSpec(memory_space=pltpu.HBM)] + [pl.BlockSpec()] * 4,
        out_specs=pl.BlockSpec(memory_space=pltpu.VMEM),
        out_shape=jax.ShapeDtypeStruct((owners, strips * slots + 8, LANES), jac.dtype),
        scratch_shapes=[pltpu.SemaphoreType.DMA((4, strips))],
        compiler_params=pltpu.CompilerParams(vmem_limit_bytes=8 << 20),
    )(*(pltpu.with_memory_space_constraint(x, pltpu.HBM) for x in (jac, frac, innov, rinv, cells)))


def observe_kernel(table, packed, depart_all, grad, spread, *, side):
    east = (side + 1) * side
    rows = table.shape[0] - east
    strips = table.shape[1] // LANES
    slots = (packed.shape[1] - 8) // strips
    tile = 2 * slots
    block = SENDERS * slots
    place = lax.broadcasted_iota(jnp.int32, (rows, tile), 0).astype(jnp.float32)

    def turn(step):
        own = packed.at[pl.ds(step * SENDERS, SENDERS)]
        depart = depart_all.at[pl.ds(step * SENDERS, SENDERS)]
        for pair in range(SENDERS // 2):
            lanes = slice(pair * tile, (pair + 1) * tile)
            meta = own[2 * pair : 2 * pair + 2, strips * slots :].astype(jnp.float32)
            fields = jnp.concatenate([meta[0], meta[1]], axis=1)
            jac = jnp.concatenate(
                [
                    own[2 * pair : 2 * pair + 2, j * slots : (j + 1) * slots].reshape(tile, LANES)
                    for j in range(strips)
                ],
                axis=1,
            )
            frac_lat, frac_lon, innov, rinv, row, col = (fields[i : i + 1] for i in range(6))
            lat_part = jnp.where(
                place == row, 1.0 - frac_lat, jnp.where(place == row + 1.0, frac_lat, 0.0)
            )
            lon_part = jnp.where(
                place == col, 1.0 - frac_lon, jnp.where(place == col + 1.0, frac_lon, 0.0)
            )
            proj = lax.dot_general(
                table[...],
                jac,
                (((1,), (1,)), ((), ())),
                preferred_element_type=jnp.float32,
            )
            bands = [
                (lat_part[i : i + 1] * lon_part[:side]).astype(jnp.bfloat16) for i in range(side + 1)
            ]
            edge = (lon_part[side : side + 1] * lat_part).astype(jnp.bfloat16)
            total = jnp.zeros((side, tile), jnp.float32)
            for i, band in enumerate(bands):
                total = total + band.astype(jnp.float32) * proj[i * side : (i + 1) * side]
            edge_total = edge.astype(jnp.float32) * proj[east:]
            evolved = jnp.sum(total, axis=0, keepdims=True) + jnp.sum(edge_total, axis=0, keepdims=True)
            departure = jnp.where(row >= 0.0, evolved - innov, 0.0)
            depart[2 * pair] = departure[:, :slots]
            depart[2 * pair + 1] = departure[:, slots:]
            scale = rinv * departure
            for i, band in enumerate(bands):
                spread[i * side : (i + 1) * side, lanes] = (band.astype(jnp.float32) * scale).astype(
                    jnp.bfloat16
                )
            spread[east:, lanes] = (edge.astype(jnp.float32) * scale).astype(jnp.bfloat16)

        jac = jnp.concatenate(
            [
                own[:, j * slots : (j + 1) * slots].reshape(block, LANES)
                for j in range(strips)
            ],
            axis=1,
        )
        part = jnp.dot(spread[...], jac, preferred_element_type=jnp.float32)
        grad[...] += part

    grad[...] = jnp.zeros_like(grad)
    lax.fori_loop(0, packed.shape[0] // SENDERS, lambda step, _: (turn(step), 0)[1], 0)


def observe(table, packed, side):
    cells, width = table.shape
    senders, slots = packed.shape[0], (packed.shape[1] - 8) * LANES // width
    block = SENDERS * slots
    whole = pl.BlockSpec(memory_space=pltpu.VMEM)
    return pl.pallas_call(
        functools.partial(observe_kernel, side=side),
        in_specs=[whole, whole],
        out_specs=[whole, whole],
        out_shape=[
            jax.ShapeDtypeStruct((senders, 1, slots), jnp.float32),
            jax.ShapeDtypeStruct((cells, width), jnp.float32),
        ],
        scratch_shapes=[pltpu.VMEM((cells, block), jnp.bfloat16)],
        compiler_params=pltpu.CompilerParams(vmem_limit_bytes=24 << 20),
    )(table, packed)


def shards(field, obs_jac, obs_frac, obs_innov, obs_rinv, obs_cells):
    side, _, width = field.shape
    stride = side + 1
    owners, _, slots, _ = obs_jac.shape
    packed = pack(
        obs_jac.reshape(owners, slots, width),
        obs_frac.reshape(owners, 2, slots),
        obs_innov.reshape(owners, slots),
        obs_rinv.reshape(owners, slots),
        obs_cells.reshape(owners, slots),
        stride,
    )
    north = shifted(field[0], "lat", -1)
    east = passed_along(jnp.concatenate([field[:, 0], north[:1]], axis=0), "lon", -1)
    pad = jnp.zeros((side - 1, width), field.dtype)
    table = jnp.concatenate([field.reshape(side * side, width), north, east, pad], axis=0)
    packed, table = lax.optimization_barrier((packed, table))
    packed = exchanged(packed)

    departs, grad = observe(table, packed, side)
    departures = exchanged(departs)
    main = side * side
    grid = grad[:main].reshape(side, side, width)
    east_back = passed_along(grad[main + side : main + 2 * side + 1], "lon", 1)
    north_row = grad[main : main + side]
    north_row = north_row + jnp.pad(east_back[side:], ((0, side - 1), (0, 0)))
    north_back = shifted(north_row, "lat", 1)
    field_grad = grid.at[:, 0].add(east_back[:side]).at[0].add(north_back)
    return (departures, field_grad)


def solution(mesh):
    placed = (
        P("lat", "lon", None),
        P(None, ("lat", "lon"), None, None),
        P(None, ("lat", "lon"), None, None),
        P(None, ("lat", "lon"), None),
        P(None, ("lat", "lon"), None),
        P(None, ("lat", "lon"), None),
    )
    return jax.shard_map(
        shards,
        mesh=mesh,
        in_specs=placed,
        out_specs=(P(None, ("lat", "lon"), None), P("lat", "lon", None)),
        check_vma=False,
    )
```

time: 209 us -> 201 us (0.962)
  starting transfers between devices: 30.1 us -> 22.2 us
  Pallas kernels: 14.2 us -> 16.8 us
    all_to_all x2 -> x1, starting transfers between devices: 17.8 us -> 9 us  [exchanged(): lax.all_to_all(block, ('lat', 'lon'), split_axis=0, concat_axis=0, tiled=...]
    pallas_call x2, Pallas kernels: 14.2 us -> 16.8 us  [the longest x1 11.2 us: observe(): pl.pallas_call(functools.partial(observe_kernel, side=side), in_specs=[wh...]
    all_to_all x2 -> x1, waiting for transfers between devices: 7.41 us -> 4.93 us  [exchanged(): lax.all_to_all(block, ('lat', 'lon'), split_axis=0, concat_axis=0, tiled=...]
  transfers between devices with their start and end apart: 6 -> 5, of which waited for: 4 -> 3; matrix products, arithmetic and copies ran while one was open for 1% -> 1% of each run, Pallas kernels for 1% -> 3%
where the time goes in v4:
time: 201 us; the launch traced here: 200 us
  blocking collectives  150 us (75%)
  starting transfers between devices  22.2 us (11%)
  Pallas kernels  16.8 us (8%)
  waiting for transfers between devices  7.38 us (4%)
  local copies, waits for them, and re-layouts  2.51 us (1%)
    all_to_all x1, blocking collectives, exchanged(): lax.all_to_all(block, ('lat', 'lon'), split_axis=0, concat_axis=0, tiled=...  150 us
    pallas_call x1, Pallas kernels, observe(): pl.pallas_call(functools.partial(observe_kernel, side=side), in_specs=[wh...  11.2 us
    all_to_all x1, starting transfers between devices, exchanged(): lax.all_to_all(block, ('lat', 'lon'), split_axis=0, concat_axis=0, tiled=...  9 us
    ppermute x2, starting transfers between devices, shifted(): return lax.ppermute(block, axis, route)  6.86 us
    ppermute x2, starting transfers between devices, passed_along(): return lax.ppermute(value, axis, pairs)  6.35 us
    pallas_call x1, Pallas kernels, pack(): pl.pallas_call(functools.partial(pack_kernel, stride=stride), in_specs=[p...  5.61 us
    all_to_all x1, waiting for transfers between devices, exchanged(): lax.all_to_all(block, ('lat', 'lon'), split_axis=0, concat_axis=0, tiled=...  4.93 us
  transfers between devices with their start and end apart: 5, of which 3 were waited for; matrix products, arithmetic and copies ran while one was open for 1% of the time, Pallas kernels for 3%

profile of v4, /device:TPU:1, one launch (start us, length us, event | category | flops | bytes accessed | tf_op | source)
XLA Modules:
  0.0 200.2 jit_solution(4339161792355111327)
XLA Ops:
  0.6 0.7 slice_bitcast_fusion
  1.3 3.3 %collective-permute-start = (bf16[16,384]{1,0:T(8,128)(2,1)S(1)}, bf16[16,384]{1,0:T(8,128)(2,1)S(1)}, u32[]{:S(2)}, u32[]{:S(2)}) collective-permute-start(bf16[16,384]{1,0:T(8,128)(2,1)S(1)} %slice_bitcast_fusion), channel_id=1, source_target_pairs={{16,0},{32,16},{48,32},{64,48},{80,64},{96,80},{112,96},{17,1},{33... | collective-permute-start | bytes 36872 | tf_op jit(solution)/shard_map/ppermute | solution.py:17
  4.7 0.9 slice.69
  5.6 0.0 copy-start.1
  5.6 1.7 collective-permute-done
  7.3 6.0 %collective-permute-start.1 = (bf16[17,384]{1,0:T(8,128)(2,1)S(1)}, bf16[17,384]{1,0:T(8,128)(2,1)S(1)}, u32[]{:S(2)}, u32[]{:S(2)}) collective-permute-start(bf16[17,384]{1,0:T(8,128)(2,1)S(1)} %pad_maximum_fusion), channel_id=1, source_target_pairs={{0,15},{1,0},{2,1},{3,2},{4,3},{5,4},{6,5},{7,6},{8,7},{9,8},{10,9... | collective-permute-start | bytes 39176 | tf_op jit(solution)/shard_map/ppermute | solution.py:23
  13.3 0.1 pad.12.clone
  13.4 5.6 %shard_map.77 = bf16[128,392,128]{2,1,0:T(8,128)(2,1)S(1)} custom-call(bf16[128,128,384]{2,1,0:T(8,128)(2,1)} %bitcast.14, bf16[128,2,128]{2,1,0:T(2,128)(2,1)} %bitcast.18, bf16[128,128]{1,0:T(8,128)(2,1)} %bitcast.21, bf16[128,128]{1,0:T(8,128)(2,1)} %bitcast.22, s32[128,128]{1,0:T(8,128)} %bitcast.19), custom_call_target="tpu_custom_call" | custom-call | tf_op jit(solution)/shard_map/pallas_call | solution.py:82
  19.0 0.0 collective-permute-done.1
  19.0 0.0 copy-done.1
  19.1 0.1 maximum_maximum_fusion.table
  19.2 150.4 %all_to_all.10.packed = bf16[128,392,128]{2,1,0:T(8,128)(2,1)S(1)} all-to-all(bf16[128,392,128]{2,1,0:T(8,128)(2,1)S(1)} %shard_map.77), channel_id=1, replica_groups=mesh['lat'=8,'lon'=16] {'lat','lon'}, dimensions={0} | all-to-all | bytes 25690112 | tf_op jit(solution)/shard_map/all_to_all | solution.py:38
  169.6 11.2 %shard_map.78 = (f32[128,1,128]{2,1,0:T(1,128)}, f32[304,384]{1,0:T(8,128)S(1)}) custom-call(bf16[304,384]{1,0:T(8,128)(2,1)S(1)} %maximum_maximum_fusion.table, bf16[128,392,128]{2,1,0:T(8,128)(2,1)S(1)} %all_to_all.10.packed), custom_call_target="tpu_custom_call" | custom-call | tf_op jit(solution)/shard_map/pallas_call | solution.py:166
  180.8 0.3 collective-permute-start.2
  181.1 9.0 %all-to-all-start.1 = ((f32[128,1,128]{2,1,0:T(1,128)}), f32[128,1,128]{2,1,0:T(1,128)S(1)}, u32[]{:S(2)}, u32[]{:S(2)}) async-start(f32[128,1,128]{2,1,0:T(1,128)} %get-tuple-element.32), calls=%async_computation.1 | async-start | bytes 131072 | tf_op jit(solution)/shard_map/all_to_all | solution.py:38
  190.2 0.0 collective-permute-done.2
  190.2 3.5 %collective-permute-start.3 = (f32[16,384]{1,0:T(8,128)S(1)}, f32[16,384]{1,0:T(8,128)S(1)}, u32[]{:S(2)}, u32[]{:S(2)}) collective-permute-start(f32[16,384]{1,0:T(8,128)S(1)} %pad_add_fusion), channel_id=1, source_target_pairs={{0,16},{16,32},{32,48},{48,64},{64,80},{80,96},{96,112},{1,17},{17... | collective-permute-start | bytes 73736 | tf_op jit(solution)/shard_map/ppermute | solution.py:17
  193.8 0.1 scatter-add.6
  193.9 0.8 collective-permute-done.3
  194.7 0.0 copy-start
  194.7 4.9 %all-to-all-done.1 = f32[128,1,128]{2,1,0:T(1,128)S(1)} async-done(((f32[128,1,128]{2,1,0:T(1,128)}), f32[128,1,128]{2,1,0:T(1,128)S(1)}, u32[]{:S(2)}, u32[]{:S(2)}) %all-to-all-start.1) | async-done | bytes 65568 | tf_op jit(solution)/shard_map/all_to_all | solution.py:38
  199.6 0.6 copy.15
  200.2 0.0 copy-done
  (11 shorter events, 0.1 us)
Async XLA Ops:
  1.3 6.0 %collective-permute-start = (bf16[16,384]{1,0:T(8,128)(2,1)S(1)}, bf16[16,384]{1,0:T(8,128)(2,1)S(1)}, u32[]{:S(2)}, u32[]{:S(2)}) collective-permute-start(bf16[16,384]{1,0:T(8,128)(2,1)S(1)} %slice_bitcast_fusion), channel_id=1, source_target_pairs={{16,0},{32,16},{48,32},{64,48},{80,64},{96,80},{112,96},{17,1},{33... | collective-permute-start | bytes 36872 | tf_op jit(solution)/shard_map/ppermute | solution.py:17
  5.6 13.5 %copy-start.1 = (bf16[16,16,384]{2,1,0:T(8,128)(2,1)S(1)}, bf16[16,16,384]{2,1,0:T(8,128)(2,1)}, u32[]{:S(2)}) copy-start(bf16[16,16,384]{2,1,0:T(8,128)(2,1)} %param.10) | copy-start | bytes 589828
  7.3 11.7 %collective-permute-start.1 = (bf16[17,384]{1,0:T(8,128)(2,1)S(1)}, bf16[17,384]{1,0:T(8,128)(2,1)S(1)}, u32[]{:S(2)}, u32[]{:S(2)}) collective-permute-start(bf16[17,384]{1,0:T(8,128)(2,1)S(1)} %pad_maximum_fusion), channel_id=1, source_target_pairs={{0,15},{1,0},{2,1},{3,2},{4,3},{5,4},{6,5},{7,6},{8,7},{9,8},{10,9... | collective-permute-start | bytes 39176 | tf_op jit(solution)/shard_map/ppermute | solution.py:23
  180.8 9.4 %collective-permute-start.2 = (f32[17,384]{1,0:T(8,128)S(1)}, f32[17,384]{1,0:T(8,128)S(1)}, u32[]{:S(2)}, u32[]{:S(2)}) collective-permute-start(f32[17,384]{1,0:T(8,128)S(1)} %slice.73), channel_id=1, source_target_pairs={{0,1},{1,2},{2,3},{3,4},{4,5},{5,6},{6,7},{7,8},{8,9},{9,10},{10,1... | collective-permute-start | bytes 78344 | tf_op jit(solution)/shard_map/ppermute | solution.py:23
  181.1 18.5 %all-to-all-start.1 = ((f32[128,1,128]{2,1,0:T(1,128)}), f32[128,1,128]{2,1,0:T(1,128)S(1)}, u32[]{:S(2)}, u32[]{:S(2)}) async-start(f32[128,1,128]{2,1,0:T(1,128)} %get-tuple-element.32), calls=%async_computation.1 | async-start | bytes 131072 | tf_op jit(solution)/shard_map/all_to_all | solution.py:38
  190.2 4.5 %collective-permute-start.3 = (f32[16,384]{1,0:T(8,128)S(1)}, f32[16,384]{1,0:T(8,128)S(1)}, u32[]{:S(2)}, u32[]{:S(2)}) collective-permute-start(f32[16,384]{1,0:T(8,128)S(1)} %pad_add_fusion), channel_id=1, source_target_pairs={{0,16},{16,32},{32,48},{48,64},{64,80},{80,96},{96,112},{1,17},{17... | collective-permute-start | bytes 73736 | tf_op jit(solution)/shard_map/ppermute | solution.py:17
  194.7 5.6 %copy-start = (f32[16,16,384]{2,1,0:T(8,128)}, f32[16,16,384]{2,1,0:T(8,128)S(1)}, u32[]{:S(2)}) copy-start(f32[16,16,384]{2,1,0:T(8,128)S(1)} %fusion) | copy-start | bytes 1179652
